TPU v7x, 128 devices: a whole 4x4x4 slice. The times are simulated.
128 devices in a mesh: section: 8 (over y, z_hi), dp: 16 (over z_lo, x, core).
Axes of the slice: x: 4, y: 4, z: 4 (z_hi: 2, z_lo: 2; z = z_hi * 2 + z_lo), core: 2. Of those that a mesh axis runs over, the one named last changes fastest.
Arguments:
- query_gradient_stack: float32 [8, 8192, 2048], P('section', 'dp'), may hold values from -6 to 6
- train_grads: float32 [8, 8192, 2048], P('section', 'dp'), may hold values from -6 to 6
- factor_slots: float32 [8, 16, 2048, 512], P('section', 'dp'), as said below
- owner: int32 [8, 4], P('section'), may hold values from 0 to 15, as said below
- train_count: int32 [16], P('dp'), may hold values from 128 to 512, as said below
Outputs:
- scores: float32 [16, 512, 1536], P('dp', 'section')
Inputs may be any that keep to these rules, and one draw needn't show every extreme that they name: `owner`: for each layer the 4 entries are distinct data indices. `train_count`: some data index has all 512 training examples live. `factor_slots`: the diagonal entries of each factor lie between 0.9 and 2.1.
All inputs are finite; a program needn't handle non-finite values.
Results may differ from a plain program's by a relative error of at most 0.00019.
Values sent between devices are 32-bit elements; how exact they have to be, the bound alone decides.
A program may use at most 128 MiB of HBM per device.

v0:
```python
import jax
import jax.numpy as jnp
from jax import lax
from jax.sharding import PartitionSpec as P

COORDS = 2048
PANEL = 512


def spread(block, axis, source):
    block = jnp.where(lax.axis_index(axis) == source, block, jnp.zeros_like(block))
    return lax.psum(block, axis)


def shifted_2(value, axis, steps):
    count = lax.axis_size(axis)
    pairs = [(source, (source + steps) % count) for source in range(count)]
    return lax.ppermute(value, axis, pairs)


def solve_rows(row_block, slot, owner_list):
    panel_count = row_block.shape[1] // PANEL
    pending = row_block
    solved_parts = []
    for panel_number in range(panel_count):
        panel_cols = spread(slot[panel_number * PANEL :, :], "dp", owner_list[panel_number])
        diag_block = jnp.tril(panel_cols[:PANEL, :])
        solved = lax.linalg.triangular_solve(
            diag_block, pending[:, :PANEL], left_side=False, lower=True, transpose_a=True
        )
        solved_parts.append(solved)
        if panel_number + 1 < panel_count:
            update = lax.dot_general(
                solved,
                panel_cols[PANEL:, :],
                (((1,), (1,)), ((), ())),
                precision=lax.Precision.HIGHEST,
                preferred_element_type=jnp.float32,
            )
            pending = pending[:, PANEL:] - update
    return jnp.concatenate(solved_parts, axis=1)


def neighbour_blocks(blocks, counts):
    gathered = []
    current = (blocks, counts)
    for step_index in range(2):
        current = shifted_2((current[0], current[1]), "dp", 1)
        gathered.append(current)
    return gathered


def body(query_gradient_stack, train_grads, factor_slots, owner, train_count):
    layer_count = query_gradient_stack.shape[0]
    row_count = query_gradient_stack.shape[1]
    score_scale = (COORDS * layer_count * lax.axis_size("section")) ** (-0.5)
    layer_index = 0
    stacked = jnp.concatenate([query_gradient_stack[layer_index], train_grads[layer_index]], axis=0)
    solved = solve_rows(stacked, factor_slots[layer_index, 0], owner[layer_index])
    query_solved = [solved[:row_count]]
    own_solved = [solved[row_count:]]
    own_stack = jnp.stack(own_solved, axis=0)
    shifted = neighbour_blocks(own_stack, train_count)
    count_list = [train_count, shifted[0][1], shifted[1][1]]
    layer_index = 0
    column_solved = [
        jnp.concatenate(
            [own_stack[layer_index], shifted[0][0][layer_index], shifted[1][0][layer_index]], axis=0
        )
    ]
    positions = jnp.arange(row_count, dtype=jnp.int32)
    valid_cols = jnp.concatenate(
        [(positions < count_item[0]).astype(jnp.float32) for count_item in count_list], axis=0
    )
    col_factor = score_scale * valid_cols
    layer_index = 0
    query_part = query_solved[layer_index]
    running = lax.dot_general(
        query_part,
        column_solved[layer_index],
        (((1,), (1,)), ((), ())),
        precision=lax.Precision.HIGHEST,
        preferred_element_type=jnp.float32,
    )
    scores = lax.psum_scatter(
        running * col_factor[None, :], "section", scatter_dimension=0, tiled=True
    )
    return scores[None]


def solution(mesh):
    in_specs = (
        P("section", "dp", None),
        P("section", "dp", None),
        P("section", "dp", None, None),
        P("section", None),
        P("dp"),
    )
    out_specs = P("dp", "section", None)
    return jax.shard_map(body, mesh=mesh, in_specs=in_specs, out_specs=out_specs, check_vma=False)
```

profile of v0, /device:TPU:0, one launch (start us, length us, event | category | flops | bytes accessed | tf_op | source)
XLA Modules:
  0.0 697.0 jit_solution(2605141269648286314)
XLA Ops:
  13.1 3.2 select_bitcast_fusion.2
  20.9 152.1 %all-reduce.3.cloned.1.call-done = (f32[2048,512]{1,0:T(8,128)}, f32[1536,512]{1,0:T(8,128)}, f32[1024,512]{1,0:T(8,128)}, f32[512,512]{1,0:T(8,128)}) async-done(((f32[2048,512]{1,0:T(8,128)}, f32[1536,512]{1,0:T(8,128)}, f32[1024,512]{1,0:T(8,128)}, f32[512,512]{1,0:T(8,128)}), (f32[2048,512]{1,0:T(8,128)}, f32[1536,512]{1,0:T(8,128)}, f32[1024,512]{1,0:T(8,128)}, ...) | async-done | bytes 10485776 | tf_op jit(solution)/shard_map/psum | solution.py:12
  173.0 3.4 select_select_fusion
  176.4 11.6 %while.11 = (s32[]{:T(128)}, f32[512,512]{1,0:T(8,128)}, s32[4,2]{0,1:T(2,128)S(1)}, f32[4,128,128]{2,1,0:T(8,128)S(1)}, s32[]{:T(128)}) while((s32[]{:T(128)}, f32[512,512]{1,0:T(8,128)}, s32[4,2]{0,1:T(2,128)S(1)}, f32[4,128,128]{2,1,0:T(8,128)S(1)}, s32[]{:T(128)}) %tuple.78), condition=%wide.while_cond.clone.2, body=%wide.while_body.clone.2.sunk | while | flops 2 | bytes 131189 | solution.py:28
  188.0 39.9 %custom-call.9 = f32[4,128,128]{1,2,0:T(8,128)} custom-call(f32[4,128,128]{2,1,0:T(8,128)S(1)} %get-tuple-element.35), custom_call_target="InvertDiagBlocksLowerTriangular" | custom-call | tf_op jit(solution)/shard_map/triangular_solve/custom-call.1 | solution.py:28
  227.9 11.6 %while.10 = (s32[]{:T(128)}, f32[512,512]{1,0:T(8,128)}, s32[4,2]{0,1:T(2,128)S(1)}, f32[4,128,128]{2,1,0:T(8,128)S(1)}, s32[]{:T(128)}) while((s32[]{:T(128)}, f32[512,512]{1,0:T(8,128)}, s32[4,2]{0,1:T(2,128)S(1)}, f32[4,128,128]{2,1,0:T(8,128)S(1)}, s32[]{:T(128)}) %tuple.86), condition=%wide.while_cond.clone.1, body=%wide.while_body.clone.1.sunk | while | flops 2 | bytes 131189 | solution.py:28
  239.6 39.9 %custom-call.8 = f32[4,128,128]{1,2,0:T(8,128)} custom-call(f32[4,128,128]{2,1,0:T(8,128)S(1)} %get-tuple-element.34), custom_call_target="InvertDiagBlocksLowerTriangular" | custom-call | tf_op jit(solution)/shard_map/triangular_solve/custom-call.1 | solution.py:28
  282.3 11.5 %while.9 = (s32[]{:T(128)}, f32[512,512]{1,0:T(8,128)}, s32[4,2]{0,1:T(2,128)S(1)}, f32[4,128,128]{2,1,0:T(8,128)S(1)}, s32[]{:T(128)}) while((s32[]{:T(128)}, f32[512,512]{1,0:T(8,128)}, s32[4,2]{0,1:T(2,128)S(1)}, f32[4,128,128]{2,1,0:T(8,128)S(1)}, s32[]{:T(128)}) %tuple.87), condition=%wide.while_cond.clone, body=%wide.while_body.clone.sunk | while | flops 2 | bytes 131189 | solution.py:28
  293.8 39.9 %custom-call.7 = f32[4,128,128]{1,2,0:T(8,128)} custom-call(f32[4,128,128]{2,1,0:T(8,128)S(1)} %get-tuple-element.33), custom_call_target="InvertDiagBlocksLowerTriangular" | custom-call | tf_op jit(solution)/shard_map/triangular_solve/custom-call.1 | solution.py:28
  333.8 11.7 %while.8 = (s32[]{:T(128)}, f32[512,512]{1,0:T(8,128)}, s32[4,2]{0,1:T(2,128)S(1)}, f32[4,128,128]{2,1,0:T(8,128)S(1)}, s32[]{:T(128)}) while((s32[]{:T(128)}, f32[512,512]{1,0:T(8,128)}, s32[4,2]{0,1:T(2,128)S(1)}, f32[4,128,128]{2,1,0:T(8,128)S(1)}, s32[]{:T(128)}) %tuple.88), condition=%wide.while_cond, body=%wide.while_body.sunk | while | flops 2 | bytes 131189 | solution.py:28
  346.2 40.3 %custom-call.6 = f32[4,128,128]{1,2,0:T(8,128)S(1)} custom-call(f32[4,128,128]{2,1,0:T(8,128)} %copy-done.10), custom_call_target="InvertDiagBlocksLowerTriangular" | custom-call | tf_op jit(solution)/shard_map/triangular_solve/custom-call.1 | solution.py:28
  396.0 3.8 fusion.72
  400.5 21.1 %fusion.6 = f32[1024,1536]{1,0:T(8,128)S(1)} fusion(f32[512,2048]{1,0:T(8,128)S(1)} %bitcast.135, f32[512,2048]{1,0:T(8,128)S(1)} %bitcast.140, f32[2048,512]{1,0:T(8,128)S(1)} %copy-done.4, f32[1024,128]{0,1:T(8,128)S(1)} %fusion.118, f32[1024,128]{0,1:T(8,128)S(1)} %fusion.119, f32[1024,128]{0,1:T(8,128)S(1)} %fusion.120, f32[1024,128]{0,1:T(8,128)S(1)} %bitcast.151), kind=kOutput, calls=%fused_computation.16 | convolution fusion | flops 9668395008 | bytes 19922944 | tf_op jit(solution)/shard_map/dot_general | solution.py:33
  428.1 3.6 fusion.69
  432.4 14.7 %slice_subtract_fusion = f32[1024,1024]{1,0:T(8,128)S(1)} fusion(f32[1024,1536]{1,0:T(8,128)S(1)} %fusion.6, f32[1536,512]{1,0:T(8,128)S(1)} %copy-done.5, f32[1024,128]{0,1:T(8,128)S(1)} %fusion.114, f32[1024,128]{0,1:T(8,128)S(1)} %fusion.115, f32[1024,128]{0,1:T(8,128)S(1)} %fusion.116, f32[1024,128]{0,1:T(8,128)S(1)} %bitcast.147), kind=kOutput, calls=%fused_computation.18 | convolution fusion | flops 6445072384 | bytes 12582912 | tf_op jit(solution)/shard_map/dot_general | solution.py:33
  453.7 3.7 fusion.66
  458.0 7.1 %slice_subtract_fusion.1 = f32[1024,512]{1,0:T(8,128)S(1)} fusion(f32[1024,1024]{1,0:T(8,128)S(1)} %slice_subtract_fusion, f32[1024,128]{0,1:T(8,128)S(1)} %fusion.110, f32[1024,128]{0,1:T(8,128)S(1)} %fusion.111, f32[1024,128]{0,1:T(8,128)S(1)} %fusion.112, f32[1024,128]{0,1:T(8,128)S(1)} %bitcast.143, f32[1024,512]{1,0:T(8,128)S(1)} %copy-done.6), kind=kOutput, calls=%fused_computation.23 | convolution fusion | flops 3223322624 | bytes 7340032 | tf_op jit(solution)/shard_map/dot_general | solution.py:33
  471.6 3.8 fusion.63
  476.9 3.3 maximum_maximum_fusion
  481.5 50.0 %collective-permute-done = f32[1,512,2048]{1,2,0:T(8,128)S(1)} collective-permute-done((f32[1,512,2048]{1,2,0:T(8,128)S(1)}, f32[1,512,2048]{1,2,0:T(8,128)S(1)}, u32[]{:S(2)}, u32[]{:S(2)}) %collective-permute-start) | collective-permute-done | bytes 4194336 | tf_op jit(solution)/shard_map/ppermute | solution.py:18
  532.4 49.4 %collective-permute-done.2 = s32[1]{0:T(128)} collective-permute-done((s32[1]{0:T(128)}, s32[1]{0:T(128)}, u32[]{:S(2)}, u32[]{:S(2)}) %collective-permute-start.2) | collective-permute-done | bytes 36 | tf_op jit(solution)/shard_map/ppermute | solution.py:18
  582.5 4.5 collective-permute-done.3
  587.6 22.8 %fusion.8 = f32[512,1536]{1,0:T(8,128)} fusion(f32[512,2048]{0,1:T(8,128)S(1)} %bitcast.157, f32[512,2048]{0,1:T(8,128)S(1)} %bitcast.156, f32[512,2048]{0,1:T(8,128)S(1)} %get-tuple-element.80, f32[1024,2048]{0,1:T(8,128)S(1)} %maximum_maximum_fusion, f32[1536]{0:T(1024)S(1)} %add_select_fusion), kind=kOutput, calls=%fused_computation.20 | convolution fusion | flops 19334430720 | bytes 19931136 | tf_op jit(solution)/shard_map/dot_general | solution.py:78
  610.5 79.3 %reduce-scatter.2.cloned.1.call-done = f32[64,1536]{1,0:T(8,128)} async-done(((f32[512,1536]{1,0:T(8,128)}), f32[64,1536]{1,0:T(8,128)}) %reduce-scatter.2.cloned.1.call-update) | async-done | bytes 393232 | tf_op jit(solution)/shard_map/reduce_scatter | solution.py:85
  (119 shorter events, 93.1 us)
Async XLA Ops:
  6.5 166.5 %all-reduce.3.cloned.1.call-start = ((), (), s32[]{:S(2)}) async-start(), calls=%async_computation.2 | async-start | bytes 20971520 | tf_op jit(solution)/shard_map/psum | solution.py:12
  10.6 5.6 copy-start.2
  20.8 668.9 %reduce-scatter.2.cloned.1.call-start = ((), (), s32[]{:S(2)}) async-start(), calls=%async_computation.1 | async-start | bytes 3538944 | tf_op jit(solution)/shard_map/reduce_scatter | solution.py:85
  173.0 106.5 %copy-start.5 = (f32[1536,512]{1,0:T(8,128)S(1)}, f32[1536,512]{1,0:T(8,128)}, u32[]{:S(2)}) copy-start(f32[1536,512]{1,0:T(8,128)} %get-tuple-element.69) | copy-start | bytes 9437188
  345.5 0.7 copy-start.10
  386.6 2.4 copy-start
  386.6 3.6 copy-start.1
  396.0 4.4 copy-start.4
  400.5 21.1 %copy-start.9 = (f32[4,128,128]{1,2,0:T(8,128)S(1)}, f32[4,128,128]{1,2,0:T(8,128)}, u32[]{:S(2)}) copy-start(f32[4,128,128]{1,2,0:T(8,128)} %custom-call.7) | copy-start | bytes 786436
  432.4 14.7 %copy-start.8 = (f32[4,128,128]{1,2,0:T(8,128)S(1)}, f32[4,128,128]{1,2,0:T(8,128)}, u32[]{:S(2)}) copy-start(f32[4,128,128]{1,2,0:T(8,128)} %custom-call.8) | copy-start | bytes 786436
  449.6 8.3 %copy-start.6 = (f32[1024,512]{1,0:T(8,128)S(1)}, f32[1024,512]{1,0:T(8,128)}, u32[]{:S(2)}) copy-start(f32[1024,512]{1,0:T(8,128)} %get-tuple-element.70) | copy-start | bytes 6291460
  457.3 7.7 %copy-start.7 = (f32[4,128,128]{1,2,0:T(8,128)S(1)}, f32[4,128,128]{1,2,0:T(8,128)}, u32[]{:S(2)}) copy-start(f32[4,128,128]{1,2,0:T(8,128)} %custom-call.9) | copy-start | bytes 786436
  471.6 3.9 copy-start.3
  481.4 50.1 %collective-permute-start = (f32[1,512,2048]{1,2,0:T(8,128)S(1)}, f32[1,512,2048]{1,2,0:T(8,128)S(1)}, u32[]{:S(2)}, u32[]{:S(2)}) collective-permute-start(f32[1,512,2048]{1,2,0:T(8,128)S(1)} %get-tuple-element.81), channel_id=1, source_target_pairs={{0,1},{1,2},{2,3},{3,4},{4,5},{5,6},{6,7},{7,8},{8,9},{9,10},{10,1... | collective-permute-start | bytes 12582920 | tf_op jit(solution)/shard_map/ppermute | solution.py:18
  531.5 56.1 %collective-permute-start.1 = (f32[1,512,2048]{1,2,0:T(8,128)S(1)}, f32[1,512,2048]{1,2,0:T(8,128)S(1)}, u32[]{:S(2)}, u32[]{:S(2)}) collective-permute-start(f32[1,512,2048]{1,2,0:T(8,128)S(1)} %collective-permute-done), channel_id=1, source_target_pairs={{0,1},{1,2},{2,3},{3,4},{4,5},{5,6},{6,7},{7,8},{8,9},{9,10},{10,1... | collective-permute-start | bytes 12582920 | tf_op jit(solution)/shard_map/ppermute | solution.py:18
  531.7 50.1 %collective-permute-start.2 = (s32[1]{0:T(128)}, s32[1]{0:T(128)}, u32[]{:S(2)}, u32[]{:S(2)}) collective-permute-start(s32[1]{0:T(128)} %param.11), channel_id=1, source_target_pairs={{0,1},{1,2},{2,3},{3,4},{4,5},{5,6},{6,7},{7,8},{8,9},{9,10},{10,1... | collective-permute-start | bytes 20 | tf_op jit(solution)/shard_map/ppermute | solution.py:18
  581.8 5.1 collective-permute-start.3
Sparse Core Ops, SparseCore 0:
  20.9 152.0 all-reduce.2
  610.6 79.0 reduce-scatter.1
where the time goes:
time: 706 us; the launch traced here: 697 us
  waiting for transfers between devices  335 us (47%)
  other arithmetic  181 us (26%)
  matrix products  111 us (16%)
  local copies, waits for them, and re-layouts  51.2 us (7%)
  between operations  17.6 us (2%)
    another operation x7, other arithmetic, solve_rows(): lax.linalg.triangular_solve(diag_block, pending[:, :PANEL], left_side=Fal...  166 us
    psum x1, waiting for transfers between devices, spread(): return lax.psum(block, axis)  152 us
    ppermute x4, waiting for transfers between devices, shifted_2(): return lax.ppermute(value, axis, pairs)  104 us
    reduce_scatter x1, waiting for transfers between devices, body(): lax.psum_scatter(running * col_factor[None, :], 'section', scatter_dimens...  79.3 us
    another operation x52, local copies, waits for them, and re-layouts, solve_rows(): lax.linalg.triangular_solve(diag_block, pending[:, :PANEL], left_side=Fal...  46.1 us
    another operation x28, matrix products, solve_rows(): lax.linalg.triangular_solve(diag_block, pending[:, :PANEL], left_side=Fal...  45.3 us
    dot_general x3, matrix products, solve_rows(): lax.dot_general(solved, panel_cols[PANEL:, :], (((1,), (1,)), ((), ())),...  42.9 us
    dot_general x1, matrix products, body(): lax.dot_general(query_part, column_solved[layer_index], (((1,), (1,)), ((...  22.8 us
  transfers between devices with their start and end apart: 6, of which 5 were waited for; matrix products, arithmetic and copies ran while one was open for 0% of the time, Pallas kernels for 0%

commit v1 on v0

v1 whole, which is shorter than its diff:
```python
import jax
import jax.numpy as jnp
from jax import lax
from jax.experimental import pallas as pl
from jax.experimental.pallas import tpu as pltpu
from jax.sharding import PartitionSpec as P

COORDS = 2048
PANEL = 512
ROWS = 512
BLOCK = 256
SMALL = 128
BASE = 16
F32, BF16 = jnp.float32, jnp.bfloat16
NT = (((1,), (1,)), ((), ()))
NN = (((1,), (0,)), ((), ()))


def split(value):
    high = value.astype(BF16)
    return high, (value - high.astype(F32)).astype(BF16)


def dot3(a_high, a_low, b_high, b_low, dims=NT):
    def one(a, b):
        return lax.dot_general(a, b, dims, preferred_element_type=F32)

    return one(a_high, b_high) + (one(a_high, b_low) + one(a_low, b_high))


def dot_f32(a, b):
    return lax.dot_general(
        a, b, NN, precision=lax.Precision.HIGHEST, preferred_element_type=F32
    )


def invert_small(block):
    row = lax.broadcasted_iota(jnp.int32, (SMALL, SMALL), 0)
    col = lax.broadcasted_iota(jnp.int32, (SMALL, SMALL), 1)
    block = jnp.where(row >= col, block, 0.0)
    diagonal = jnp.sum(jnp.where(row == col, block, 0.0), axis=1, keepdims=True)
    scale = (1.0 / diagonal).reshape(SMALL // BASE, BASE, 1)
    inner = jnp.where(row // BASE == col // BASE, block, 0.0)
    inverse = jnp.where(row == col, 1.0, 0.0).reshape(SMALL // BASE, BASE, SMALL)
    place = lax.broadcasted_iota(jnp.int32, inverse.shape, 1)
    for step in range(BASE):
        factor = jnp.sum(jnp.where(col % BASE == step, inner, 0.0), axis=1, keepdims=True)
        factor = factor.reshape(SMALL // BASE, BASE, 1)
        pivot = inverse[:, step : step + 1, :] * scale[:, step : step + 1, :]
        below = inverse - jnp.where(place > step, factor, 0.0) * pivot
        inverse = jnp.where(place == step, pivot, below)
    inverse = inverse.reshape(SMALL, SMALL)
    size = BASE
    while size < SMALL:
        left = (row // size) % 2 == 1
        pick = left & (col // size == row // size - 1)
        inner = dot_f32(jnp.where(pick, block, 0.0), inverse)
        inverse = inverse - dot_f32(inverse, inner)
        size *= 2
    return inverse


def solve_kernel(
    q_hbm, t_hbm, p0, p1, p2, p3, count_ref, x_ref,
    l_high, l_low, x_high, x_low, w_high, w_low, diag, copy_sem,
):
    panels = (p0, p1, p2, p3)
    copies = [
        pltpu.make_async_copy(source, x_ref.at[index], copy_sem.at[index])
        for index, source in enumerate((q_hbm, t_hbm))
    ]
    for copy in copies:
        copy.start()
    for number, panel in enumerate(panels):
        first = number * PANEL
        for part in range(PANEL // SMALL):
            at = part * SMALL
            diag[number * (PANEL // SMALL) + part] = panel[at : at + SMALL, at : at + SMALL]

        @pl.loop(0, (COORDS - first) // BLOCK)
        def _(step):
            rows = pl.ds(pl.multiple_of(step * BLOCK, BLOCK), BLOCK)
            there = pl.ds(pl.multiple_of(first + step * BLOCK, BLOCK), BLOCK)
            high, low = split(panel[rows, :])
            l_high[there, first : first + PANEL] = high
            l_low[there, first : first + PANEL] = low

    @pl.loop(0, COORDS // SMALL // 4)
    def _(step):
        for index in range(4):
            diag[step * 4 + index] = invert_small(diag[step * 4 + index])

    w_high[...] = jnp.zeros_like(w_high)
    w_low[...] = jnp.zeros_like(w_low)
    for block in range(COORDS // BLOCK):
        panel, at = panels[block // 2], (block % 2) * BLOCK
        upper, lower = diag[2 * block], diag[2 * block + 1]
        cross = panel[at + SMALL : at + BLOCK, at : at + SMALL]
        corner = -dot_f32(lower, dot_f32(cross, upper))
        base = block * BLOCK
        for value, rows, cols in ((upper, 0, 0), (corner, SMALL, 0), (lower, SMALL, SMALL)):
            high, low = split(value)
            w_high[base + rows : base + rows + SMALL, cols : cols + SMALL] = high
            w_low[base + rows : base + rows + SMALL, cols : cols + SMALL] = low

    for copy in copies:
        copy.wait()
    for block in range(COORDS // BLOCK):
        base = block * BLOCK
        cols = slice(base, base + BLOCK)

        @pl.loop(0, 2)
        def _(half):
            pending = x_ref[half, :, cols]
            if block:
                pending = pending - dot3(
                    x_high[half, :, :base], x_low[half, :, :base], l_high[cols, :base], l_low[cols, :base]
                )
            high, low = split(pending)
            solved = dot3(high, low, w_high[cols, :], w_low[cols, :])
            x_ref[half, :, cols] = solved
            high, low = split(solved)
            x_high[half, :, cols] = high
            x_low[half, :, cols] = low

    place = lax.broadcasted_iota(jnp.int32, (ROWS, SMALL), 0)
    keep = jnp.where(place < count_ref[0], F32(1.0 / 128.0), F32(0.0))
    for part in range(COORDS // SMALL):
        cols = slice(part * SMALL, (part + 1) * SMALL)
        x_ref[1, :, cols] = x_ref[1, :, cols] * keep


def solve(query, train, panels, count):
    vmem, anyspace = pl.BlockSpec(memory_space=pltpu.VMEM), pl.BlockSpec(memory_space=pl.ANY)
    return pl.pallas_call(
        solve_kernel,
        out_shape=jax.ShapeDtypeStruct((2, ROWS, COORDS), F32),
        in_specs=[anyspace] * 2 + [vmem] * 4 + [pl.BlockSpec(memory_space=pltpu.SMEM)],
        out_specs=vmem,
        scratch_shapes=[
            pltpu.VMEM((COORDS, COORDS), BF16),
            pltpu.VMEM((COORDS, COORDS), BF16),
            pltpu.VMEM((2, ROWS, COORDS), BF16),
            pltpu.VMEM((2, ROWS, COORDS), BF16),
            pltpu.VMEM((COORDS, BLOCK), BF16),
            pltpu.VMEM((COORDS, BLOCK), BF16),
            pltpu.VMEM((COORDS // SMALL, SMALL, SMALL), F32),
            pltpu.SemaphoreType.DMA((2,)),
        ],
        compiler_params=pltpu.CompilerParams(vmem_limit_bytes=60 << 20),
        name="solve",
    )(query, train, *panels, count)


def spread(block, axis, source):
    block = jnp.where(lax.axis_index(axis) == source, block, jnp.zeros_like(block))
    return lax.psum(block, axis)


def score(left, right):
    return lax.dot_general(
        left, right, NT, precision=lax.Precision.HIGH, preferred_element_type=F32
    )


def body(query_gradient_stack, train_grads, factor_slots, owner, train_count):
    count = lax.axis_size("dp")
    me = lax.axis_index("dp")
    even = me % 2 == 0
    slot, owners = factor_slots[0, 0], owner[0]
    panels = [spread(slot[j * PANEL :], "dp", owners[j]) for j in range(COORDS // PANEL)]
    solved = solve(query_gradient_stack[0], train_grads[0], panels, train_count)
    query, train = solved[0], solved[1]
    evens = range(0, count, 2)
    before = lax.ppermute(train, "dp", [(d, (d + 1) % count) for d in range(count)])
    later_query = lax.ppermute(query, "dp", [((d + 2) % count, d) for d in evens])
    before_that = lax.ppermute(before, "dp", [(d, d + 1) for d in evens])
    first = score(query, train)
    second = score(query, before)
    third = score(jnp.where(even, later_query, query), jnp.where(even, train, before_that))
    tiles = jnp.concatenate([first, second, third], axis=1)
    summed = lax.psum_scatter(tiles, "section", scatter_dimension=0, tiled=True)
    last = summed[:, 2 * ROWS :]
    moved = lax.ppermute(last, "dp", [(d, (d + 2) % count) for d in evens])
    return jnp.concatenate([summed[:, : 2 * ROWS], jnp.where(even, moved, last)], axis=1)[None]


def solution(mesh):
    in_specs = (
        P("section", "dp", None),
        P("section", "dp", None),
        P("section", "dp", None, None),
        P("section", None),
        P("dp"),
    )
    out_specs = P("dp", "section", None)
    return jax.shard_map(body, mesh=mesh, in_specs=in_specs, out_specs=out_specs, check_vma=False)
```

time: 706 us -> 407 us (0.58); the launches traced: 697 us -> 406 us
  other arithmetic: 181 us -> 10.5 us
  matrix products: 111 us -> 18.2 us
  Pallas kernels: 0 us -> 53.1 us
  waiting for transfers between devices: 335 us -> 282 us
  local copies, waits for them, and re-layouts: 51.2 us -> 14.3 us
  starting transfers between devices: 0.4 us -> 11.6 us
    another operation x7 -> x0, other arithmetic: 166 us -> none  [solve_rows(): lax.linalg.triangular_solve(diag_block, pending[:, :PANEL], left_side=Fal...]
    reduce_scatter x1 -> x0, waiting for transfers between devices: 79.3 us -> none  [body(): lax.psum_scatter(running * col_factor[None, :], 'section', scatter_dimens...]
    unnamed x2 -> x3, waiting for transfers between devices: 0.03 us -> 79.2 us
    pallas_call x0 -> x1, Pallas kernels: none -> 53.1 us  [solve(): pl.pallas_call(solve_kernel, out_shape=jax.ShapeDtypeStruct((2, ROWS, COO...]
    ppermute x4, waiting for transfers between devices: 104 us -> 51 us  [the longest x1 45.2 us: body(): lax.ppermute(train, 'dp', [(d, (d + 1) % count) for d in range(count)])]
    dot_general x4 -> x3, matrix products: 65.7 us -> 18.2 us  [score(): lax.dot_general(left, right, NT, precision=lax.Precision.HIGH, preferred_...]
    another operation x52 -> x0, local copies, waits for them, and re-layouts: 46.1 us -> none  [solve_rows(): lax.linalg.triangular_solve(diag_block, pending[:, :PANEL], left_side=Fal...]
    another operation x28 -> x0, matrix products: 45.3 us -> none  [solve_rows(): lax.linalg.triangular_solve(diag_block, pending[:, :PANEL], left_side=Fal...]
  transfers between devices with their start and end apart: 6 -> 6, of which waited for: 5 -> 4; matrix products, arithmetic and copies ran while one was open for 0% -> 3% of each run, Pallas kernels for 0% -> 0%
where the time goes in v1:
time: 407 us; the launch traced here: 406 us
  waiting for transfers between devices  282 us (69%)
  Pallas kernels  53.1 us (13%)
  matrix products  18.2 us (4%)
  between operations  16.7 us (4%)
  local copies, waits for them, and re-layouts  14.3 us (4%)
  starting transfers between devices  11.6 us (3%)
  other arithmetic  10.5 us (3%)
    psum x1, waiting for transfers between devices, spread(): return lax.psum(block, axis)  151 us
    unnamed x3, waiting for transfers between devices  79.2 us
    pallas_call x1, Pallas kernels, solve(): pl.pallas_call(solve_kernel, out_shape=jax.ShapeDtypeStruct((2, ROWS, COO...  53.1 us
    ppermute x1, waiting for transfers between devices, body(): lax.ppermute(train, 'dp', [(d, (d + 1) % count) for d in range(count)])  45.2 us
    dot_general x3, matrix products, score(): lax.dot_general(left, right, NT, precision=lax.Precision.HIGH, preferred_...  18.2 us
    select_n x4, other arithmetic, spread(): jnp.where(lax.axis_index(axis) == source, block, jnp.zeros_like(block))  10.1 us
  transfers between devices with their start and end apart: 6, of which 4 were waited for; matrix products, arithmetic and copies ran while one was open for 3% of the time, Pallas kernels for 0%

profile of v1, /device:TPU:0, one launch (start us, length us, event | category | flops | bytes accessed | tf_op | source)
XLA Modules:
  0.0 406.1 jit_solution(7571139158171066102)
XLA Ops:
  6.5 1.5 fusion.6
  9.3 2.6 select_bitcast_fusion
  11.9 1.0 copy-done.1
  13.0 2.0 select_bitcast_fusion.1
  15.6 3.1 select_bitcast_fusion.2
  19.4 2.3 select_bitcast_fusion.3
  22.4 151.5 %all-reduce.3.cloned.1.call-done = (f32[2048,512]{1,0:T(8,128)}, f32[1536,512]{1,0:T(8,128)}, f32[1024,512]{1,0:T(8,128)}, f32[512,512]{1,0:T(8,128)}) async-done(((f32[2048,512]{1,0:T(8,128)}, f32[1536,512]{1,0:T(8,128)}, f32[1024,512]{1,0:T(8,128)}, f32[512,512]{1,0:T(8,128)}), (f32[2048,512]{1,0:T(8,128)}, f32[1536,512]{1,0:T(8,128)}, f32[1024,512]{1,0:T(8,128)}, ...) | async-done | bytes 10485776 | tf_op jit(solution)/shard_map/psum | solution.py:157
  173.9 53.1 %solve.1 = f32[2,512,2048]{2,1,0:T(8,128)} custom-call(f32[512,2048]{1,0:T(8,128)} %bitcast.31, f32[512,2048]{1,0:T(8,128)} %bitcast.32, f32[2048,512]{1,0:T(8,128)} %get-tuple-element.5.p0, f32[1536,512]{1,0:T(8,128)} %get-tuple-element.6.p1, f32[1024,512]{1,0:T(8,128)} %get-tuple-element.7.p2, f32[512,512]{1,0:T(8,128)} %get-tuple-element.8.p3, ...), custom_call_target="tpu_custom_call" | custom-call | tf_op jit(solution)/shard_map/solve/pallas_call | solution.py:135
  227.0 6.3 %slice_bitcast_fusion.1 = (f32[512,2048]{1,0:T(8,128)}, f32[512,2048]{1,0:T(8,128)S(1)}) fusion(f32[2,512,2048]{2,1,0:T(8,128)} %solve.1), kind=kLoop, calls=%fused_computation.1 | loop fusion | bytes 16777216 | tf_op jit(solution)/shard_map/squeeze | solution.py:173
  233.3 4.9 %collective-permute-start.1 = (f32[512,2048]{1,0:T(8,128)}, f32[512,2048]{1,0:T(8,128)}, u32[]{:S(2)}, u32[]{:S(2)}) collective-permute-start(f32[512,2048]{1,0:T(8,128)} %get-tuple-element.9), channel_id=1, source_target_pairs={{2,0},{4,2},{6,4},{8,6},{10,8},{12,10},{14,12},{0,14},{18,16},{20,... | collective-permute-start | bytes 12582920 | tf_op jit(solution)/shard_map/ppermute | solution.py:176
  238.3 45.2 %collective-permute-done = f32[512,2048]{1,0:T(8,128)} collective-permute-done((f32[512,2048]{1,0:T(8,128)S(1)}, f32[512,2048]{1,0:T(8,128)}, u32[]{:S(2)}, u32[]{:S(2)}) %collective-permute-start) | collective-permute-done | bytes 4194336 | tf_op jit(solution)/shard_map/ppermute | solution.py:175
  283.5 3.2 collective-permute-start.2
  286.7 6.8 %fusion.4 = f32[512,512]{0,1:T(8,128)S(1)} fusion(f32[2,512,2048]{2,1,0:T(8,128)} %solve.1), kind=kOutput, calls=%fused_computation.13 | convolution fusion | flops 3221225472 | bytes 9437184 | tf_op jit(solution)/shard_map/dot_general | solution.py:161
  293.6 5.4 %fusion.5 = f32[512,512]{0,1:T(8,128)S(1)} fusion(f32[512,2048]{1,0:T(8,128)} %collective-permute-done, f32[2,512,2048]{2,1,0:T(8,128)S(1)} %copy-done), kind=kOutput, calls=%fused_computation.14 | convolution fusion | flops 3221225472 | bytes 9437184 | tf_op jit(solution)/shard_map/dot_general | solution.py:161
  299.0 5.9 %fusion = f32[512,512]{0,1:T(8,128)S(1)} fusion(f32[512,2048]{1,0:T(8,128)} %collective-permute-done.2, f32[512,2048]{1,0:T(8,128)} %collective-permute-done.1, pred[]{:T(512)S(6)} %eq.21, f32[2,512,2048]{2,1,0:T(8,128)S(1)} %copy-done), kind=kOutput, calls=%fused_computation.2 | convolution fusion | flops 3223322624 | bytes 17826816 | tf_op jit(solution)/shard_map/dot_general | solution.py:161
  304.9 0.3 pad_maximum_fusion
  305.2 2.3 copy.8
  307.6 79.2 %reduce-scatter.4.cloned.1.call-done = f32[64,1536]{1,0:T(8,128)} async-done(((f32[512,1536]{1,0:T(8,128)}), f32[64,1536]{1,0:T(8,128)}) %reduce-scatter.4.cloned.1.call-update) | async-done | bytes 393232
  386.8 0.9 slice.54
  387.8 3.4 collective-permute-start.3
  391.3 1.0 slice.53
  392.2 0.2 copy.10
  392.4 5.8 %collective-permute-done.3 = f32[64,512]{0,1:T(8,128)S(1)} collective-permute-done((f32[64,512]{0,1:T(8,128)S(1)}, f32[64,512]{0,1:T(8,128)S(1)}, u32[]{:S(2)}, u32[]{:S(2)}) %collective-permute-start.3) | collective-permute-done | bytes 131104 | tf_op jit(solution)/shard_map/ppermute | solution.py:184
  398.3 1.0 copy.7
  (13 shorter events, 0.3 us)
Async XLA Ops:
  6.5 167.4 %all-reduce.3.cloned.1.call-start = ((), (), s32[]{:S(2)}) async-start(), calls=%async_computation.2 | async-start | bytes 20971520 | tf_op jit(solution)/shard_map/psum | solution.py:157
  9.3 3.7 copy-start.1
  21.7 365.0 %reduce-scatter.4.cloned.1.call-start = ((), (), s32[]{:S(2)}) async-start(), calls=%async_computation.1 | async-start | bytes 3538944
  233.3 50.1 %collective-permute-start = (f32[512,2048]{1,0:T(8,128)S(1)}, f32[512,2048]{1,0:T(8,128)}, u32[]{:S(2)}, u32[]{:S(2)}) collective-permute-start(f32[512,2048]{1,0:T(8,128)S(1)} %get-tuple-element.10), channel_id=1, source_target_pairs={{0,1},{1,2},{2,3},{3,4},{4,5},{5,6},{6,7},{7,8},{8,9},{9,10},{10,1... | collective-permute-start | bytes 12582920 | tf_op jit(solution)/shard_map/ppermute | solution.py:175
  233.3 65.6 %collective-permute-start.1 = (f32[512,2048]{1,0:T(8,128)}, f32[512,2048]{1,0:T(8,128)}, u32[]{:S(2)}, u32[]{:S(2)}) collective-permute-start(f32[512,2048]{1,0:T(8,128)} %get-tuple-element.9), channel_id=1, source_target_pairs={{2,0},{4,2},{6,4},{8,6},{10,8},{12,10},{14,12},{0,14},{18,16},{20,... | collective-permute-start | bytes 12582920 | tf_op jit(solution)/shard_map/ppermute | solution.py:176
  283.5 15.5 %collective-permute-start.2 = (f32[512,2048]{1,0:T(8,128)}, f32[512,2048]{1,0:T(8,128)}, u32[]{:S(2)}, u32[]{:S(2)}) collective-permute-start(f32[512,2048]{1,0:T(8,128)} %collective-permute-done), channel_id=1, source_target_pairs={{0,1},{2,3},{4,5},{6,7},{8,9},{10,11},{12,13},{14,15},{16,17},{18,... | collective-permute-start | bytes 12582920 | tf_op jit(solution)/shard_map/ppermute | solution.py:177
  286.7 6.8 %copy-start = (f32[2,512,2048]{2,1,0:T(8,128)S(1)}, f32[2,512,2048]{2,1,0:T(8,128)}, u32[]{:S(2)}) copy-start(f32[2,512,2048]{2,1,0:T(8,128)} %solve.1) | copy-start | bytes 25165828
  387.8 10.4 %collective-permute-start.3 = (f32[64,512]{0,1:T(8,128)S(1)}, f32[64,512]{0,1:T(8,128)S(1)}, u32[]{:S(2)}, u32[]{:S(2)}) collective-permute-start(f32[64,512]{0,1:T(8,128)S(1)} %copy.11), channel_id=1, source_target_pairs={{0,2},{2,4},{4,6},{6,8},{8,10},{10,12},{12,14},{14,0},{16,18},{18,... | collective-permute-start | bytes 393224 | tf_op jit(solution)/shard_map/ppermute | solution.py:184
Sparse Core Ops, SparseCore 0:
  21.9 152.0 all-reduce.2
  307.7 79.0 reduce-scatter.3

commit v2 on v1

v2 whole, which is shorter than its diff:
```python
import jax
import jax.numpy as jnp
from jax import lax
from jax.experimental import pallas as pl
from jax.experimental.pallas import tpu as pltpu
from jax.sharding import PartitionSpec as P

COORDS = 2048
PANEL = 512
ROWS = 512
BLOCK = 256
SMALL = 128
BASE = 16
F32, BF16 = jnp.float32, jnp.bfloat16
NT = (((1,), (1,)), ((), ()))
NN = (((1,), (0,)), ((), ()))
MESH = pl.DeviceIdType.MESH
PANELS = COORDS // PANEL
CHUNK = 128
PART = 16


def split(value):
    high = value.astype(BF16)
    return high, (value - high.astype(F32)).astype(BF16)


def dot3(a_high, a_low, b_high, b_low, dims=NT):
    def one(a, b):
        return lax.dot_general(a, b, dims, preferred_element_type=F32)

    return one(a_high, b_high) + (one(a_high, b_low) + one(a_low, b_high))


def dot_f32(a, b):
    return lax.dot_general(
        a, b, NN, precision=lax.Precision.HIGHEST, preferred_element_type=F32
    )


def invert_small(block):
    row = lax.broadcasted_iota(jnp.int32, (SMALL, SMALL), 0)
    col = lax.broadcasted_iota(jnp.int32, (SMALL, SMALL), 1)
    block = jnp.where(row >= col, block, 0.0)
    diagonal = jnp.sum(jnp.where(row == col, block, 0.0), axis=1, keepdims=True)
    scale = (1.0 / diagonal).reshape(SMALL // BASE, BASE, 1)
    inner = jnp.where(row // BASE == col // BASE, block, 0.0)
    inverse = jnp.where(row == col, 1.0, 0.0).reshape(SMALL // BASE, BASE, SMALL)
    place = lax.broadcasted_iota(jnp.int32, inverse.shape, 1)
    for step in range(BASE):
        factor = jnp.sum(jnp.where(col % BASE == step, inner, 0.0), axis=1, keepdims=True)
        factor = factor.reshape(SMALL // BASE, BASE, 1)
        pivot = inverse[:, step : step + 1, :] * scale[:, step : step + 1, :]
        below = inverse - jnp.where(place > step, factor, 0.0) * pivot
        inverse = jnp.where(place == step, pivot, below)
    inverse = inverse.reshape(SMALL, SMALL)
    size = BASE
    while size < SMALL:
        left = (row // size) % 2 == 1
        pick = left & (col // size == row // size - 1)
        inner = dot_f32(jnp.where(pick, block, 0.0), inverse)
        inverse = inverse - dot_f32(inverse, inner)
        size *= 2
    return inverse


def load_factor(panels, stage, stage_sem, l_high, l_low, diag, cross):
    pieces = [(group, number) for group in range(PANELS) for number in range(group + 1)]

    def fetch(index):
        group, number = pieces[index]
        rows = pl.ds((group - number) * PANEL, PANEL)
        slot = index % 2
        return pltpu.make_async_copy(panels[number].at[rows, :], stage.at[slot], stage_sem.at[slot])

    fetch(0).start()
    for index, (group, number) in enumerate(pieces):
        if index + 1 < len(pieces):
            fetch(index + 1).start()
        fetch(index).wait()
        slot = index % 2
        cols = slice(number * PANEL, (number + 1) * PANEL)

        @pl.loop(0, PANEL // CHUNK)
        def _(step):
            high, low = split(stage[slot, pl.ds(pl.multiple_of(step * CHUNK, CHUNK), CHUNK), :])
            there = pl.ds(pl.multiple_of(group * PANEL + step * CHUNK, CHUNK), CHUNK)
            l_high[there, cols] = high
            l_low[there, cols] = low

        if group == number:
            for part in range(PANEL // SMALL):
                at = slice(part * SMALL, (part + 1) * SMALL)
                diag[group * (PANEL // SMALL) + part] = stage[slot, at, at]
            for part in range(PANEL // BLOCK):
                at = part * BLOCK
                cross[group * (PANEL // BLOCK) + part] = stage[
                    slot, at + SMALL : at + BLOCK, at : at + SMALL
                ]


def invert_blocks(diag, cross, w_high, w_low):
    @pl.loop(0, COORDS // SMALL // 4)
    def _(step):
        for index in range(4):
            diag[step * 4 + index] = invert_small(diag[step * 4 + index])

    w_high[...] = jnp.zeros_like(w_high)
    w_low[...] = jnp.zeros_like(w_low)

    @pl.loop(0, COORDS // BLOCK // 2)
    def _(step):
        for index in range(2):
            block = step * 2 + index
            upper, lower = diag[2 * block], diag[2 * block + 1]
            corner = -dot_f32(lower, dot_f32(cross[block], upper))
            for value, rows, cols in ((upper, 0, 0), (corner, SMALL, 0), (lower, SMALL, SMALL)):
                high, low = split(value)
                there = pl.ds(pl.multiple_of(block * BLOCK + rows, SMALL), SMALL)
                w_high[there, cols : cols + SMALL] = high
                w_low[there, cols : cols + SMALL] = low


def solve_half(half, x_ref, x_high, x_low, l_high, l_low, w_high, w_low):
    for block in range(COORDS // BLOCK):
        base = block * BLOCK
        cols = slice(base, base + BLOCK)
        pending = x_ref[half, :, cols]
        if block:
            pending = pending - dot3(
                x_high[half, :, :base], x_low[half, :, :base], l_high[cols, :base], l_low[cols, :base]
            )
        high, low = split(pending)
        solved = dot3(high, low, w_high[cols, :], w_low[cols, :])
        x_ref[half, :, cols] = solved
        high, low = split(solved)
        x_high[half, :, cols] = high
        x_low[half, :, cols] = low


def score_kernel(
    q_hbm, t_hbm, p0, p1, p2, p3, count_ref, out_ref,
    l_high, l_low, x_ref, x_high, x_low, w_high, w_low, diag, cross, stage,
    a_in, b_in, c_high, c_low, tiles, first_in, second_out, second_in, kept, third_out, third_in,
    load_sem, stage_sem, a_send, a_recv, b_send, b_recv, r_send,
    f_send, f_recv, s_send, s_recv, m_send, m_recv,
):
    me, section = lax.axis_index("dp"), lax.axis_index("section")
    count = lax.axis_size("dp")
    rings, row_of, half_of = 4, section // 2, section % 2
    even = me % 2 == 0
    odd = me % 2 == 1
    after, before = lax.rem(me + 1, count), lax.rem(me + count - 1, count)
    after_two, before_two = lax.rem(me + 2, count), lax.rem(me + count - 2, count)

    def section_at(steps):
        return lax.rem(row_of + steps, rings) * 2 + half_of

    partner = row_of * 2 + 1 - half_of
    barrier = pltpu.get_barrier_semaphore()
    for other in (after, before, after_two, before_two):
        pl.semaphore_signal(barrier, inc=1, device_id={"dp": other}, device_id_type=MESH)
    for other in (section_at(1), section_at(2), section_at(3), partner):
        pl.semaphore_signal(barrier, inc=1, device_id={"section": other}, device_id_type=MESH)

    copies = [
        pltpu.make_async_copy(source, x_ref.at[index], load_sem.at[index])
        for index, source in enumerate((q_hbm, t_hbm))
    ]
    for copy in copies:
        copy.start()
    load_factor((p0, p1, p2, p3), stage, stage_sem, l_high, l_low, diag, cross)
    for copy in copies:
        copy.wait()
    place = lax.broadcasted_iota(jnp.int32, (ROWS, SMALL), 0)
    keep = jnp.where(place < count_ref[0], F32(1.0 / 128.0), F32(0.0))
    for part in range(COORDS // SMALL):
        cols = slice(part * SMALL, (part + 1) * SMALL)
        x_ref[1, :, cols] = x_ref[1, :, cols] * keep
    invert_blocks(diag, cross, w_high, w_low)
    pl.semaphore_wait(barrier, 8)

    def remote(source, target, send, recv, where):
        return pltpu.make_async_remote_copy(
            src_ref=source, dst_ref=target, send_sem=send, recv_sem=recv,
            device_id=where, device_id_type=MESH,
        )

    def send_train(part):
        rows = pl.ds(pl.multiple_of(part * CHUNK, CHUNK), CHUNK)
        return remote(x_ref.at[1, rows, :], a_in.at[part], a_send.at[part], a_recv.at[part], {"dp": after})

    def send_query(part, piece):
        rows = pl.ds(pl.multiple_of(piece * 64 + part * PART, PART), PART)
        there = pl.ds(piece * PART, PART)
        return remote(
            x_ref.at[0, rows, :], b_in.at[part, there, :], b_send.at[part], b_recv.at[part], {"dp": before_two}
        )

    def relay(part):
        return remote(a_in.at[part], b_in.at[part], r_send.at[part], b_recv.at[part], {"dp": after})

    @pl.loop(0, 2)
    def _(step):
        half = lax.rem(step + me, 2)
        solve_half(half, x_ref, x_high, x_low, l_high, l_low, w_high, w_low)

        @pl.when(half == 1)
        def _():
            for part in range(4):
                send_train(part).start()

        @pl.when((half == 0) & even)
        def _():
            for part in range(4):
                for piece in range(8):
                    send_query(part, piece).start()

    def chunk(part):
        return pl.ds(pl.multiple_of(part * CHUNK, CHUNK), CHUNK)

    def small_rows(part, base):
        return pl.ds(pl.multiple_of(base + part * PART, PART), PART)

    def first_column(tile, part, steps):
        to = lax.rem(row_of + steps, rings)
        rows = pl.ds(pl.multiple_of(to * 128, 128), 128)
        at = tile * 4 + part
        return remote(
            tiles.at[tile, rows, chunk(part)], first_in.at[tile, steps - 1, :, chunk(part)],
            f_send.at[at, steps - 1], f_recv.at[at, steps - 1], {"section": section_at(steps)},
        )

    def first_row(part, steps, side):
        to = lax.rem(row_of + steps, rings)
        at = 8 + part
        return remote(
            tiles.at[2, small_rows(part, to * 128 + side * 64), :],
            first_in.at[2, steps - 1, small_rows(part, side * 64), :],
            f_send.at[at, steps - 1], f_recv.at[at, steps - 1], {"section": section_at(steps)},
        )

    def column_piece(tile, part, high, low):
        tiles[tile, :, chunk(part)] = dot3(x_high[0], x_low[0], high, low)
        for steps in (1, 2, 3):
            first_column(tile, part, steps).start()

    def first_waits(tile, part):
        for steps in (1, 2, 3):
            first_column(tile, part, steps).wait()

    def sum_columns(tile, part):
        first_waits(tile, part)
        for mine in (True, False):
            side = half_of if mine else 1 - half_of
            there = pl.ds(pl.multiple_of(side * 64, 64), 64)
            rows = pl.ds(pl.multiple_of(row_of * 128 + side * 64, 64), 64)
            total = tiles[tile, rows, chunk(part)]
            for steps in range(3):
                total = total + first_in[tile, steps, there, chunk(part)]
            if mine:
                kept[tile, :, chunk(part)] = total
            else:
                second_out[tile, :, chunk(part)] = total
        second_column(tile, part).start()

    def second_column(tile, part):
        at = tile * 4 + part
        return remote(
            second_out.at[tile, :, chunk(part)], second_in.at[tile, :, chunk(part)],
            s_send.at[at], s_recv.at[at], {"section": partner},
        )

    def end_columns(tile, part):
        second_column(tile, part).wait()
        there = pl.ds(pl.multiple_of(tile * ROWS + part * CHUNK, CHUNK), CHUNK)
        out_ref[:, there] = kept[tile, :, chunk(part)] + second_in[tile, :, chunk(part)]

    def sum_rows(part):
        first_waits(2, part)
        for mine in (True, False):
            side = half_of if mine else 1 - half_of
            total = tiles[2, small_rows(part, row_of * 128 + side * 64), :]
            for steps in range(3):
                total = total + first_in[2, steps, small_rows(part, side * 64), :]
            if mine:
                kept[2, small_rows(part, 0), :] = total
            else:
                second_out[2, small_rows(part, 0), :] = total
        second_row(part).start()

    def second_row(part):
        at = 8 + part
        return remote(
            second_out.at[2, small_rows(part, 0), :], second_in.at[2, small_rows(part, 0), :],
            s_send.at[at], s_recv.at[at], {"section": partner},
        )

    def move(part):
        return remote(
            third_out.at[small_rows(part, 0), :], third_in.at[small_rows(part, 0), :],
            m_send.at[part], m_recv.at[part], {"dp": after_two},
        )

    def end_rows(part):
        second_row(part).wait()
        rows = small_rows(part, 0)
        third_out[rows, :] = kept[2, rows, :] + second_in[2, rows, :]
        move(part).start()

    @pl.loop(0, 4)
    def _(part):
        column_piece(0, part, x_high[1, chunk(part), :], x_low[1, chunk(part), :])

    @pl.loop(0, 7)
    def _(step):
        @pl.when(step < 4)
        def _():
            send_train(step).wait()

            @pl.when(even)
            def _():
                relay(step).start()

            c_high[...], c_low[...] = split(a_in[step])
            column_piece(1, step, c_high[...], c_low[...])
            pltpu.make_async_copy(b_in.at[step], b_in.at[step], b_recv.at[step]).wait()
            c_high[...], c_low[...] = split(b_in[step])

            @pl.when(odd)
            def _():
                column_piece(2, step, c_high[...], c_low[...])

            @pl.when(even)
            def _():
                made = dot3(c_high[...], c_low[...], x_high[1], x_low[1])
                for piece in range(8):
                    tiles[2, small_rows(step, piece * 64), :] = made[piece * PART : (piece + 1) * PART]
                for steps in (1, 2, 3):
                    for side in range(2):
                        first_row(step, steps, side).start()

            sum_columns(0, step)

        @pl.when((step >= 1) & (step < 5))
        def _():
            sum_columns(1, step - 1)

            @pl.when(odd)
            def _():
                sum_columns(2, step - 1)

            @pl.when(even)
            def _():
                sum_rows(step - 1)

            end_columns(0, step - 1)

        @pl.when((step >= 2) & (step < 6))
        def _():
            end_columns(1, step - 2)

            @pl.when(odd)
            def _():
                end_columns(2, step - 2)

            @pl.when(even)
            def _():
                end_rows(step - 2)

        @pl.when((step >= 3) & even)
        def _():
            move(step - 3).wait()
            out_ref[small_rows(step - 3, 0), 2 * ROWS :] = third_in[small_rows(step - 3, 0), :]

    @pl.when(even)
    def _():
        for part in range(4):
            relay(part).wait_send()
            pltpu.make_async_copy(b_in.at[part], b_in.at[part], b_send.at[part]).wait()


def scores_of(query, train, panels, count):
    vmem, anyspace = pl.BlockSpec(memory_space=pltpu.VMEM), pl.BlockSpec(memory_space=pl.ANY)
    dma = pltpu.SemaphoreType.DMA
    return pl.pallas_call(
        score_kernel,
        out_shape=jax.ShapeDtypeStruct((64, 3 * ROWS), F32),
        in_specs=[anyspace] * 6 + [pl.BlockSpec(memory_space=pltpu.SMEM)],
        out_specs=vmem,
        scratch_shapes=[
            pltpu.VMEM((COORDS, COORDS), BF16),
            pltpu.VMEM((COORDS, COORDS), BF16),
            pltpu.VMEM((2, ROWS, COORDS), F32),
            pltpu.VMEM((2, ROWS, COORDS), BF16),
            pltpu.VMEM((2, ROWS, COORDS), BF16),
            pltpu.VMEM((COORDS, BLOCK), BF16),
            pltpu.VMEM((COORDS, BLOCK), BF16),
            pltpu.VMEM((COORDS // SMALL, SMALL, SMALL), F32),
            pltpu.VMEM((COORDS // BLOCK, SMALL, SMALL), F32),
            pltpu.VMEM((2, PANEL, PANEL), F32),
            pltpu.VMEM((4, CHUNK, COORDS), F32),
            pltpu.VMEM((4, CHUNK, COORDS), F32),
            pltpu.VMEM((CHUNK, COORDS), BF16),
            pltpu.VMEM((CHUNK, COORDS), BF16),
            pltpu.VMEM((3, ROWS, ROWS), F32),
            pltpu.VMEM((3, 3, 128, ROWS), F32),
            pltpu.VMEM((3, 64, ROWS), F32),
            pltpu.VMEM((3, 64, ROWS), F32),
            pltpu.VMEM((3, 64, ROWS), F32),
            pltpu.VMEM((64, ROWS), F32),
            pltpu.VMEM((64, ROWS), F32),
            dma((2,)), dma((2,)), dma((4,)), dma((4,)), dma((4,)), dma((4,)), dma((4,)),
            dma((12, 3)), dma((12, 3)), dma((12,)), dma((12,)), dma((4,)), dma((4,)),
        ],
        compiler_params=pltpu.CompilerParams(
            vmem_limit_bytes=63 << 20, collective_id=0, has_side_effects=True
        ),
        name="scores",
    )(query, train, *panels, count)


def spread(block, axis, source):
    block = jnp.where(lax.axis_index(axis) == source, block, jnp.zeros_like(block))
    return lax.psum(block, axis)


def body(query_gradient_stack, train_grads, factor_slots, owner, train_count):
    slot, owners = factor_slots[0, 0], owner[0]
    panels = [spread(slot[j * PANEL :], "dp", owners[j]) for j in range(PANELS)]
    return scores_of(query_gradient_stack[0], train_grads[0], panels, train_count)[None]


def solution(mesh):
    in_specs = (
        P("section", "dp", None),
        P("section", "dp", None),
        P("section", "dp", None, None),
        P("section", None),
        P("dp"),
    )
    out_specs = P("dp", "section", None)
    return jax.shard_map(body, mesh=mesh, in_specs=in_specs, out_specs=out_specs, check_vma=False)
```

time: 407 us -> 306 us (0.75)
  waiting for transfers between devices: 282 us -> 152 us
  Pallas kernels: 53.1 us -> 123 us
  matrix products: 18.2 us -> 0 us
  starting transfers between devices: 11.6 us -> 0.01 us
  local copies, waits for them, and re-layouts: 14.3 us -> 4.28 us
    unnamed x3 -> x1, waiting for transfers between devices: 79.2 us -> 0.02 us
    pallas_call x1, Pallas kernels: 53.1 us -> 123 us  [scores_of(): pl.pallas_call(score_kernel, out_shape=jax.ShapeDtypeStruct((64, 3 * ROWS...]
    ppermute x4 -> x0, waiting for transfers between devices: 51 us -> none  [the longest x1 45.2 us: body(): lax.ppermute(train, 'dp', [(d, (d + 1) % count) for d in range(count)])]
    dot_general x3 -> x0, matrix products: 18.2 us -> none  [score(): lax.dot_general(left, right, NT, precision=lax.Precision.HIGH, preferred_...]
    ppermute x4 -> x0, starting transfers between devices: 11.6 us -> none  [the longest x1 4.92 us: body(): lax.ppermute(query, 'dp', [((d + 2) % count, d) for d in evens])]
    squeeze x1 -> x0, local copies, waits for them, and re-layouts: 6.29 us -> none  [body(): query, train = (solved[0], solved[1])]
  transfers between devices with their start and end apart: 6 -> 1, of which waited for: 4 -> 1; matrix products, arithmetic and copies ran while one was open for 3% -> 0% of each run, Pallas kernels for 0% -> 0%
where the time goes in v2:
time: 306 us
  waiting for transfers between devices  152 us (50%)
  Pallas kernels  123 us (40%)
  between operations  16.6 us (5%)
  other arithmetic  10.2 us (3%)
  local copies, waits for them, and re-layouts  4.28 us (1%)
    psum x1, waiting for transfers between devices, spread(): return lax.psum(block, axis)  152 us
    pallas_call x1, Pallas kernels, scores_of(): pl.pallas_call(score_kernel, out_shape=jax.ShapeDtypeStruct((64, 3 * ROWS...  123 us
    select_n x4, other arithmetic, spread(): jnp.where(lax.axis_index(axis) == source, block, jnp.zeros_like(block))  10.2 us
  transfers between devices with their start and end apart: 1, of which 1 were waited for; matrix products, arithmetic and copies ran while one was open for 0% of the time, Pallas kernels for 0%

profile of v2, /device:TPU:0, one launch (start us, length us, event | category | flops | bytes accessed | tf_op | source)
XLA Modules:
  0.0 305.7 jit_solution(14547872884249542275)
XLA Ops:
  6.5 0.0 all-reduce.3.cloned.1.call-start
  6.5 1.5 fusion
  9.2 0.0 copy-start
  9.2 2.6 select_bitcast_fusion
  11.8 1.0 copy-done
  12.9 2.1 select_bitcast_fusion.1
  15.7 3.1 %select_bitcast_fusion.2 = f32[1024,512]{1,0:T(8,128)} fusion(f32[1,1,2048,512]{3,2,1,0:T(8,128)} %param.7, pred[]{:T(512)S(6)} %eq.14), kind=kLoop, calls=%fused_computation.2 | loop fusion | flops 524288 | bytes 4194305 | tf_op jit(solution)/shard_map/jit(_where)/select_n | solution.py:424
  19.5 2.3 select_bitcast_fusion.3
  21.8 0.0 all-reduce.3.cloned.1.call-update
  22.4 152.2 %all-reduce.3.cloned.1.call-done = (f32[2048,512]{1,0:T(8,128)}, f32[1536,512]{1,0:T(8,128)}, f32[1024,512]{1,0:T(8,128)}, f32[512,512]{1,0:T(8,128)}) async-done(((f32[2048,512]{1,0:T(8,128)}, f32[1536,512]{1,0:T(8,128)}, f32[1024,512]{1,0:T(8,128)}, f32[512,512]{1,0:T(8,128)}), (f32[2048,512]{1,0:T(8,128)}, f32[1536,512]{1,0:T(8,128)}, f32[1024,512]{1,0:T(8,128)}, ...) | async-done | bytes 10485776 | tf_op jit(solution)/shard_map/psum | solution.py:425
  174.6 122.5 %scores.1 = f32[64,1536]{1,0:T(8,128)} custom-call(f32[512,2048]{1,0:T(8,128)} %bitcast.15, f32[512,2048]{1,0:T(8,128)} %bitcast.16, f32[2048,512]{1,0:T(8,128)} %get-tuple-element.5.p0, f32[1536,512]{1,0:T(8,128)} %get-tuple-element.6.p1, f32[1024,512]{1,0:T(8,128)} %get-tuple-element.7.p2, f32[512,512]{1,0:T(8,128)} %get-tuple-element.8.p3, ...), custom_call_target="tpu_custom_call" | custom-call | tf_op jit(solution)/shard_map/scores/pallas_call | solution.py:386
  297.1 1.8 copy.12
Async XLA Ops:
  6.5 168.1 %all-reduce.3.cloned.1.call-start = ((), (), s32[]{:S(2)}) async-start(), calls=%async_computation | async-start | bytes 20971520 | tf_op jit(solution)/shard_map/psum | solution.py:425
  9.2 3.7 %copy-start = (f32[1,1,2048,512]{3,2,1,0:T(8,128)S(1)}, f32[1,1,2048,512]{3,2,1,0:T(8,128)}, u32[]{:S(2)}) copy-start(f32[1,1,2048,512]{3,2,1,0:T(8,128)} %param.7) | copy-start | bytes 12582916
Sparse Core Ops, SparseCore 0:
  21.9 152.6 all-reduce.2

commit v3 on v2

v3 whole, which is shorter than its diff:
```python
import jax
import jax.numpy as jnp
from jax import lax
from jax.experimental import pallas as pl
from jax.experimental.pallas import tpu as pltpu
from jax.sharding import PartitionSpec as P

COORDS = 2048
PANEL = 512
ROWS = 512
BLOCK = 256
SMALL = 128
BASE = 16
F32, BF16 = jnp.float32, jnp.bfloat16
NT = (((1,), (1,)), ((), ()))
NN = (((1,), (0,)), ((), ()))
MESH = pl.DeviceIdType.MESH
PANELS = COORDS // PANEL
CHUNK = 128
PART = 16
PEERS = 16
STRIP = PANEL // PEERS
Z_ROWS = STRIP // 2
PIECES = [group * (group + 1) // 2 for group in range(PANELS + 1)]


def split(value):
    high = value.astype(BF16)
    return high, (value - high.astype(F32)).astype(BF16)


def dot3(a_high, a_low, b_high, b_low, dims=NT):
    def one(a, b):
        return lax.dot_general(a, b, dims, preferred_element_type=F32)

    return one(a_high, b_high) + (one(a_high, b_low) + one(a_low, b_high))


def invert_small(blocks):
    row = lax.broadcasted_iota(jnp.int32, (SMALL, SMALL), 0)
    col = lax.broadcasted_iota(jnp.int32, (SMALL, SMALL), 1)
    groups = (SMALL // BASE, BASE)

    def substituted(block):
        diagonal = jnp.sum(jnp.where(row == col, block, 0.0), axis=1, keepdims=True)
        scale = (1.0 / diagonal).reshape(*groups, 1)
        inner = jnp.where(row // BASE == col // BASE, block, 0.0)
        inverse = jnp.where(row == col, 1.0, 0.0).reshape(*groups, SMALL)
        place = lax.broadcasted_iota(jnp.int32, inverse.shape, 1)
        for step in range(BASE):
            factor = jnp.sum(jnp.where(col % BASE == step, inner, 0.0), axis=1, keepdims=True)
            factor = jnp.where(place > step, factor.reshape(*groups, 1), 0.0)
            pivot = inverse[:, step : step + 1, :] * scale[:, step : step + 1, :]
            inverse = jnp.where(place == step, pivot, inverse - factor * pivot)
        return inverse.reshape(SMALL, SMALL)

    inverses = [substituted(block) for block in blocks]
    size = BASE
    while size < SMALL:
        pick = ((row // size) % 2 == 1) & (col // size == row // size - 1)
        halves = [split(inverse) for inverse in inverses]
        inner = [
            split(dot3(*split(jnp.where(pick, block, 0.0)), high, low, NN))
            for block, (high, low) in zip(blocks, halves)
        ]
        inverses = [
            inverse - dot3(*half, *middle, NN)
            for inverse, half, middle in zip(inverses, halves, inner)
        ]
        size *= 2
    return inverses


def load_group(group, factor, stage, stage_sem, l_high, l_low, w_high, w_low):
    def fetch(number):
        slot = number % 2
        return pltpu.make_async_copy(factor.at[PIECES[group] + number], stage.at[slot], stage_sem.at[slot])

    def strips(slot, first, rows, cols):
        part = stage[slot, first // STRIP : (first + rows) // STRIP, :, cols]
        return part.reshape(rows, part.shape[-1])

    fetch(0).start()
    for number in range(group + 1):
        if number < group:
            fetch(number + 1).start()
        fetch(number).wait()
        cols = slice(number * PANEL, (number + 1) * PANEL)

        @pl.loop(0, PANEL // CHUNK)
        def _(step):
            part = stage[number % 2, pl.ds(step * (CHUNK // STRIP), CHUNK // STRIP)]
            high, low = split(part.reshape(CHUNK, PANEL))
            there = pl.ds(pl.multiple_of(group * PANEL + step * CHUNK, CHUNK), CHUNK)
            l_high[there, cols] = high
            l_low[there, cols] = low

    slot = group % 2
    inverses = invert_small(
        [strips(slot, at, SMALL, slice(at, at + SMALL)) for at in range(0, PANEL, SMALL)]
    )
    for part in range(PANEL // BLOCK):
        at = part * BLOCK
        upper, lower = inverses[2 * part], inverses[2 * part + 1]
        cross = strips(slot, at + SMALL, SMALL, slice(at, at + SMALL))
        corner = -dot3(*split(lower), *split(dot3(*split(cross), *split(upper), NN)), NN)
        base = group * PANEL + at
        blank = jnp.zeros((SMALL, SMALL), F32)
        for value, rows, cols in ((upper, 0, 0), (corner, SMALL, 0), (lower, SMALL, SMALL), (blank, 0, SMALL)):
            high, low = split(value)
            w_high[base + rows : base + rows + SMALL, cols : cols + SMALL] = high
            w_low[base + rows : base + rows + SMALL, cols : cols + SMALL] = low


def solve_group(group, half, x_ref, x_high, x_low, l_high, l_low, w_high, w_low):
    base = group * PANEL
    cols = slice(base, base + PANEL)
    pending = x_ref[half, :, cols]
    if group:
        pending = pending - dot3(
            x_high[half, :, :base], x_low[half, :, :base], l_high[cols, :base], l_low[cols, :base]
        )
    for number in range(PANEL // BLOCK):
        at = base + number * BLOCK
        here, known = slice(at, at + BLOCK), slice(base, at)
        part = pending[:, number * BLOCK : (number + 1) * BLOCK]
        if number:
            part = part - dot3(
                x_high[half, :, known], x_low[half, :, known], l_high[here, known], l_low[here, known]
            )
        high, low = split(part)
        solved = dot3(high, low, w_high[here, :], w_low[here, :])
        x_ref[half, :, here] = solved
        high, low = split(solved)
        x_high[half, :, here] = high
        x_low[half, :, here] = low


def device_at(z, x, core):
    return lax.rem(z, 2) * 8 + lax.rem(x, 4) * 2 + lax.rem(core, 2)


ROLES = (
    "z", "left", "right", "far_lo", "far_hi", "z_left_z", "z_right_z", "z_left_x", "z_right_x",
    "z_far_lo", "z_far_hi", "z_far_x",
) + tuple("core%d" % number for number in range(8))
SENDS = 24
ALL, Z_PART, X_PART = (0, STRIP), (0, Z_ROWS), (Z_ROWS, STRIP - Z_ROWS)
FULL, LOW, HIGH = (0, PANEL), (0, PANEL // 2), (PANEL // 2, PANEL // 2)


class Exchange:
    def __init__(self, slot, owner, factor, gathered, mine, sems):
        self.slot, self.owner, self.factor, self.gathered, self.mine = slot, owner, factor, gathered, mine
        self.spread_send, self.spread_recv, self.local, self.pass_send, self.pass_recv = sems
        me = self.me = lax.axis_index("dp")
        self.z, self.x, self.core = z, x, core = me // 8, (me // 2) % 4, me % 2
        order = ((1, 0), (0, 1), (1, 3), (0, 2), (1, 1), (0, 3), (1, 2), (0, 0))
        self.peers = [
            device_at(z + dz, x + dx, core + dc) for dz, dx in order for dc in (0, 1) if dz or dx or dc
        ]
        self.z_peer, self.other = device_at(z + 1, x, core), device_at(z, x, core + 1)
        self.right, self.left = device_at(z, x + 1, core), device_at(z, x + 3, core)
        self.far = device_at(z, x + 2, core)
        self.z_left, self.z_right = device_at(z + 1, x + 3, core), device_at(z + 1, x + 1, core)
        self.z_far = device_at(z + 1, x + 2, core)
        self.started = [[] for _ in range(PANELS)]

    def remote(self, source, target, send, recv, where):
        return pltpu.make_async_remote_copy(
            src_ref=source, dst_ref=target, send_sem=send, recv_sem=recv,
            device_id={"dp": where}, device_id_type=MESH,
        )

    def spread(self, group):
        for number, to in enumerate(self.peers):
            yield self.remote(
                self.slot.at[group, to], self.gathered[group].at[self.me],
                self.spread_send.at[group, number], self.spread_recv.at[group, number], to,
            )
        yield pltpu.make_async_copy(
            self.slot.at[group, self.me], self.gathered[group].at[self.me], self.local.at[group]
        )

    def spread_start(self, group):
        for copy in self.spread(group):
            copy.start()

    def spread_wait(self, group):
        for copy in self.spread(group):
            copy.wait()
        for number in range(group + 1):
            self.mine[PIECES[group] + number] = self.gathered[group][self.owner[0, number]]

    def pieces(self, group):
        return slice(PIECES[group], PIECES[group + 1])

    def keep_own(self, group):
        return pltpu.make_async_copy(
            self.mine.at[self.pieces(group)], self.factor.at[self.pieces(group), self.me],
            self.local.at[PANELS + group],
        )

    def send(self, group, role, who, rows, cols, where, source=None):
        at = (self.pieces(group), who, pl.ds(*rows), pl.ds(*cols))
        source = self.factor.at[at] if source is None else source
        number = len(self.started[group])
        self.remote(
            source, self.factor.at[at], self.pass_send.at[group, number],
            self.pass_recv.at[group, ROLES.index(role)], where,
        ).start()
        self.started[group].append((rows, cols))

    def wait(self, group, sem, rows, cols):
        view = self.factor.at[self.pieces(group), self.me, pl.ds(*rows), pl.ds(*cols)]
        pltpu.make_async_copy(view, view, sem).wait()

    def recv(self, group, role, rows=ALL, cols=FULL):
        self.wait(group, self.pass_recv.at[group, ROLES.index(role)], rows, cols)

    def stage_0(self, group):
        own = self.mine.at[self.pieces(group)]
        for role, where in (("z", self.z_peer), ("left", self.right), ("right", self.left), ("core0", self.other)):
            self.send(group, role, self.me, ALL, FULL, where, own)
        self.keep_own(group).start()

    def stage_1(self, group):
        self.recv(group, "z")
        self.send(group, "z_left_z", self.z_peer, Z_PART, FULL, self.right)
        self.send(group, "z_right_z", self.z_peer, Z_PART, FULL, self.left)
        self.send(group, "core1", self.z_peer, ALL, FULL, self.other)
        self.recv(group, "left")
        self.send(group, "far_lo", self.left, ALL, LOW, self.right)
        self.send(group, "z_left_x", self.left, X_PART, FULL, self.z_peer)
        self.send(group, "core2", self.left, ALL, FULL, self.other)
        self.recv(group, "right")
        self.send(group, "far_hi", self.right, ALL, HIGH, self.left)
        self.send(group, "z_right_x", self.right, X_PART, FULL, self.z_peer)
        self.send(group, "core3", self.right, ALL, FULL, self.other)

    def stage_2(self, group):
        self.recv(group, "far_lo", ALL, LOW)
        self.recv(group, "far_hi", ALL, HIGH)
        self.send(group, "z_far_x", self.far, X_PART, FULL, self.z_peer)
        self.send(group, "core4", self.far, ALL, FULL, self.other)
        self.recv(group, "z_left_z", Z_PART)
        self.send(group, "z_far_lo", self.z_left, Z_PART, LOW, self.right)
        self.recv(group, "z_right_z", Z_PART)
        self.send(group, "z_far_hi", self.z_right, Z_PART, HIGH, self.left)
        self.recv(group, "z_left_x", X_PART)
        self.send(group, "core5", self.z_left, ALL, FULL, self.other)
        self.recv(group, "z_right_x", X_PART)
        self.send(group, "core6", self.z_right, ALL, FULL, self.other)

    def stage_3(self, group):
        self.recv(group, "z_far_lo", Z_PART, LOW)
        self.recv(group, "z_far_hi", Z_PART, HIGH)
        self.recv(group, "z_far_x", X_PART)
        self.send(group, "core7", self.z_far, ALL, FULL, self.other)

    def arrived(self, group):
        for number in range(8):
            self.recv(group, "core%d" % number)
        self.keep_own(group).wait()

    def drain(self):
        for group in range(PANELS):
            for number, (rows, cols) in enumerate(self.started[group]):
                self.wait(group, self.pass_send.at[group, number], rows, cols)


def score_kernel(
    q_hbm, t_hbm, slot_hbm, owner_ref, count_ref, out_ref, factor,
    gather_0, gather_1, gather_2, gather_3, mine,
    l_high, l_low, x_ref, x_high, x_low, w_high, w_low, stage,
    a_in, b_in, tiles, first_in, second_out, second_in, kept, third_out, third_in,
    load_sem, stage_sem, a_send, a_recv, b_send, b_recv, r_send,
    f_send, f_recv, s_send, s_recv, m_send, m_recv, *pass_sems,
):
    me, section = lax.axis_index("dp"), lax.axis_index("section")
    count = lax.axis_size("dp")
    rings, row_of, half_of = 4, section // 2, section % 2
    even = me % 2 == 0
    odd = me % 2 == 1
    after, before_two = lax.rem(me + 1, count), lax.rem(me + count - 2, count)
    after_two = lax.rem(me + 2, count)
    exchange = Exchange(
        slot_hbm, owner_ref, factor, (gather_0, gather_1, gather_2, gather_3), mine, pass_sems
    )

    def section_at(steps):
        return lax.rem(row_of + steps, rings) * 2 + half_of

    partner = row_of * 2 + 1 - half_of
    barrier = pltpu.get_barrier_semaphore()
    for other in exchange.peers:
        pl.semaphore_signal(barrier, inc=1, device_id={"dp": other}, device_id_type=MESH)
    for other in (section_at(1), section_at(2), section_at(3), partner):
        pl.semaphore_signal(barrier, inc=1, device_id={"section": other}, device_id_type=MESH)

    copies = [
        pltpu.make_async_copy(source, x_ref.at[index], load_sem.at[index])
        for index, source in enumerate((q_hbm, t_hbm))
    ]
    for copy in copies:
        copy.start()
    pl.semaphore_wait(barrier, len(exchange.peers) + 4)
    exchange.spread_start(0)
    exchange.spread_start(1)
    for copy in copies:
        copy.wait()
    place = lax.broadcasted_iota(jnp.int32, (ROWS, SMALL), 0)
    keep = jnp.where(place < count_ref[0], F32(1.0 / 128.0), F32(0.0))
    for part in range(COORDS // SMALL):
        cols = slice(part * SMALL, (part + 1) * SMALL)
        x_ref[1, :, cols] = x_ref[1, :, cols] * keep

    def remote(source, target, send, recv, where):
        return pltpu.make_async_remote_copy(
            src_ref=source, dst_ref=target, send_sem=send, recv_sem=recv,
            device_id=where, device_id_type=MESH,
        )

    whole, early, last = pl.ds(0, ROWS), slice(0, COORDS - PANEL), pl.ds(COORDS - PANEL, PANEL)

    def chunk(part):
        return pl.ds(pl.multiple_of(part * CHUNK, CHUNK), CHUNK)

    def small_rows(part, base):
        return pl.ds(pl.multiple_of(base + part * PART, PART), PART)

    def group_cols(group):
        return pl.ds(group * PANEL, PANEL)

    def send_train(at, rows, cols):
        return remote(x_ref.at[1, rows, cols], a_in.at[rows, cols], a_send.at[at], a_recv.at[at], {"dp": after})

    def send_query(at, rows, cols):
        return remote(x_ref.at[0, rows, cols], b_in.at[rows, cols], b_send.at[at], b_recv.at[at], {"dp": before_two})

    def relay(at, rows, cols):
        return remote(a_in.at[rows, cols], b_in.at[rows, cols], r_send.at[at], b_recv.at[at], {"dp": after})

    def shift_group(group):
        send_train(group, whole, group_cols(group)).start()

        @pl.when(even)
        def _():
            send_query(group, whole, group_cols(group)).start()

    def relay_group(group):
        send_train(group, whole, group_cols(group)).wait_recv()

        @pl.when(even)
        def _():
            relay(group, whole, group_cols(group)).start()

    def load(group):
        load_group(group, factor, stage, stage_sem, l_high, l_low, w_high, w_low)

    def solve(group, half):
        solve_group(group, half, x_ref, x_high, x_low, l_high, l_low, w_high, w_low)

    def solve_both(group):
        @pl.loop(0, 2)
        def _(half):
            solve(group, half)

    for group in range(PANELS):
        exchange.spread_wait(group)
        exchange.stage_0(group)
        if group + 2 < PANELS:
            exchange.spread_start(group + 2)
        if group >= 1:
            exchange.stage_1(group - 1)
        if group >= 2:
            exchange.stage_2(group - 2)
        if group >= 3:
            exchange.stage_3(group - 3)
    exchange.arrived(0)
    load(0)
    solve_both(0)
    exchange.stage_1(3)
    exchange.stage_2(2)
    exchange.stage_3(1)
    shift_group(0)
    exchange.arrived(1)
    load(1)
    exchange.stage_2(3)
    exchange.stage_3(2)
    solve_both(1)
    exchange.stage_3(3)
    shift_group(1)
    exchange.arrived(2)
    load(2)
    solve_both(2)
    shift_group(2)
    exchange.arrived(3)
    load(3)

    @pl.loop(0, 2)
    def _(step):
        half = lax.rem(step + me, 2)
        solve(3, half)

        @pl.when(half == 1)
        def _():
            for part in range(4):
                send_train(3 + part, chunk(part), last).start()

        @pl.when((half == 0) & even)
        def _():
            for part in range(4):
                for piece in range(8):
                    send_query(3 + part, small_rows(part, piece * 64), last).start()

    def first_column(tile, part, steps):
        to = lax.rem(row_of + steps, rings)
        rows = pl.ds(pl.multiple_of(to * 128, 128), 128)
        at = tile * 4 + part
        return remote(
            tiles.at[tile, rows, chunk(part)], first_in.at[tile, steps - 1, :, chunk(part)],
            f_send.at[at, steps - 1], f_recv.at[at, steps - 1], {"section": section_at(steps)},
        )

    def first_row(part, steps, side):
        to = lax.rem(row_of + steps, rings)
        at = 8 + part
        return remote(
            tiles.at[2, small_rows(part, to * 128 + side * 64), :],
            first_in.at[2, steps - 1, small_rows(part, side * 64), :],
            f_send.at[at, steps - 1], f_recv.at[at, steps - 1], {"section": section_at(steps)},
        )

    def column_piece(tile, part, source):
        high, low = split(source[chunk(part), last])
        tiles[tile, :, chunk(part)] += dot3(x_high[0, :, last], x_low[0, :, last], high, low)
        for steps in (1, 2, 3):
            first_column(tile, part, steps).start()

    def keep_split(source, base):
        @pl.loop(0, ROWS // CHUNK)
        def _(part):
            high, low = split(source[chunk(part), early])
            there = pl.ds(pl.multiple_of(base + part * CHUNK, CHUNK), CHUNK)
            l_high[there, early] = high
            l_low[there, early] = low

    def first_waits(tile, part):
        for steps in (1, 2, 3):
            first_column(tile, part, steps).wait()

    def sum_columns(tile, part):
        first_waits(tile, part)
        for mine in (True, False):
            side = half_of if mine else 1 - half_of
            there = pl.ds(pl.multiple_of(side * 64, 64), 64)
            rows = pl.ds(pl.multiple_of(row_of * 128 + side * 64, 64), 64)
            total = tiles[tile, rows, chunk(part)]
            for steps in range(3):
                total = total + first_in[tile, steps, there, chunk(part)]
            if mine:
                kept[tile, :, chunk(part)] = total
            else:
                second_out[tile, :, chunk(part)] = total
        second_column(tile, part).start()

    def second_column(tile, part):
        at = tile * 4 + part
        return remote(
            second_out.at[tile, :, chunk(part)], second_in.at[tile, :, chunk(part)],
            s_send.at[at], s_recv.at[at], {"section": partner},
        )

    def end_columns(tile, part):
        second_column(tile, part).wait()
        there = pl.ds(pl.multiple_of(tile * ROWS + part * CHUNK, CHUNK), CHUNK)
        out_ref[:, there] = kept[tile, :, chunk(part)] + second_in[tile, :, chunk(part)]

    def sum_rows(part):
        first_waits(2, part)
        for mine in (True, False):
            side = half_of if mine else 1 - half_of
            total = tiles[2, small_rows(part, row_of * 128 + side * 64), :]
            for steps in range(3):
                total = total + first_in[2, steps, small_rows(part, side * 64), :]
            if mine:
                kept[2, small_rows(part, 0), :] = total
            else:
                second_out[2, small_rows(part, 0), :] = total
        second_row(part).start()

    def second_row(part):
        at = 8 + part
        return remote(
            second_out.at[2, small_rows(part, 0), :], second_in.at[2, small_rows(part, 0), :],
            s_send.at[at], s_recv.at[at], {"section": partner},
        )

    def move(part):
        return remote(
            third_out.at[small_rows(part, 0), :], third_in.at[small_rows(part, 0), :],
            m_send.at[part], m_recv.at[part], {"dp": after_two},
        )

    def end_rows(part):
        second_row(part).wait()
        rows = small_rows(part, 0)
        third_out[rows, :] = kept[2, rows, :] + second_in[2, rows, :]
        move(part).start()

    relay_group(0)
    relay_group(1)
    tiles[0] = dot3(x_high[0], x_low[0], x_high[1], x_low[1])
    for part in range(4):
        for steps in (1, 2, 3):
            first_column(0, part, steps).start()
    relay_group(2)
    keep_split(a_in, 0)
    tiles[1] = dot3(x_high[0, :, early], x_low[0, :, early], l_high[:ROWS, early], l_low[:ROWS, early])
    for group in range(PANELS - 1):
        view = b_in.at[whole, group_cols(group)]
        pltpu.make_async_copy(view, view, b_recv.at[group]).wait()
    keep_split(b_in, ROWS)
    second = slice(ROWS, 2 * ROWS)

    @pl.when(odd)
    def _():
        tiles[2] = dot3(x_high[0, :, early], x_low[0, :, early], l_high[second, early], l_low[second, early])

    @pl.when(even)
    def _():
        tiles[2] = dot3(l_high[second, early], l_low[second, early], x_high[1, :, early], x_low[1, :, early])

    @pl.loop(0, 7)
    def _(step):
        @pl.when(step < 4)
        def _():
            send_train(3 + step, chunk(step), last).wait()

            @pl.when(even)
            def _():
                relay(3 + step, chunk(step), last).start()

            column_piece(1, step, a_in)
            view = b_in.at[chunk(step), last]
            pltpu.make_async_copy(view, view, b_recv.at[3 + step]).wait()

            @pl.when(odd)
            def _():
                column_piece(2, step, b_in)

            @pl.when(even)
            def _():
                rows = [b_in[small_rows(step, piece * 64), last] for piece in range(8)]
                high, low = split(jnp.concatenate(rows, axis=0))
                made = dot3(high, low, x_high[1, :, last], x_low[1, :, last])
                for piece in range(8):
                    tiles[2, small_rows(step, piece * 64), :] += made[piece * PART : (piece + 1) * PART]
                for steps in (1, 2, 3):
                    for side in range(2):
                        first_row(step, steps, side).start()

            sum_columns(0, step)

        @pl.when((step >= 1) & (step < 5))
        def _():
            sum_columns(1, step - 1)

            @pl.when(odd)
            def _():
                sum_columns(2, step - 1)

            @pl.when(even)
            def _():
                sum_rows(step - 1)

            end_columns(0, step - 1)

        @pl.when((step >= 2) & (step < 6))
        def _():
            end_columns(1, step - 2)

            @pl.when(odd)
            def _():
                end_columns(2, step - 2)

            @pl.when(even)
            def _():
                end_rows(step - 2)

        @pl.when((step >= 3) & even)
        def _():
            move(step - 3).wait()
            out_ref[small_rows(step - 3, 0), 2 * ROWS :] = third_in[small_rows(step - 3, 0), :]

    @pl.when(even)
    def _():
        for group in range(PANELS - 1):
            relay(group, whole, group_cols(group)).wait_send()
            send_query(group, whole, group_cols(group)).wait_send()
        for part in range(4):
            relay(3 + part, chunk(part), last).wait_send()
            view = b_in.at[chunk(part), last]
            pltpu.make_async_copy(view, view, b_send.at[3 + part]).wait()

    for group in range(PANELS - 1):
        send_train(group, whole, group_cols(group)).wait_send()

    exchange.drain()


def scores_of(query, train, slot, owner, count):
    vmem, anyspace = pl.BlockSpec(memory_space=pltpu.VMEM), pl.BlockSpec(memory_space=pl.ANY)
    smem = pl.BlockSpec(memory_space=pltpu.SMEM)
    dma = pltpu.SemaphoreType.DMA
    scores, _ = pl.pallas_call(
        score_kernel,
        out_shape=(
            jax.ShapeDtypeStruct((64, 3 * ROWS), F32),
            jax.ShapeDtypeStruct((PIECES[-1], PEERS, STRIP, PANEL), F32),
        ),
        in_specs=[anyspace] * 3 + [smem] * 2,
        out_specs=(vmem, anyspace),
        scratch_shapes=[pltpu.VMEM((PEERS, STRIP, PANEL), F32)] * PANELS
        + [
            pltpu.VMEM((PIECES[-1], STRIP, PANEL), F32),
            pltpu.VMEM((COORDS, COORDS), BF16),
            pltpu.VMEM((COORDS, COORDS), BF16),
            pltpu.VMEM((2, ROWS, COORDS), F32),
            pltpu.VMEM((2, ROWS, COORDS), BF16),
            pltpu.VMEM((2, ROWS, COORDS), BF16),
            pltpu.VMEM((COORDS, BLOCK), BF16),
            pltpu.VMEM((COORDS, BLOCK), BF16),
            pltpu.VMEM((2, PEERS, STRIP, PANEL), F32),
            pltpu.VMEM((ROWS, COORDS), F32),
            pltpu.VMEM((ROWS, COORDS), F32),
            pltpu.VMEM((3, ROWS, ROWS), F32),
            pltpu.VMEM((3, 3, 128, ROWS), F32),
            pltpu.VMEM((3, 64, ROWS), F32),
            pltpu.VMEM((3, 64, ROWS), F32),
            pltpu.VMEM((3, 64, ROWS), F32),
            pltpu.VMEM((64, ROWS), F32),
            pltpu.VMEM((64, ROWS), F32),
            dma((2,)), dma((2,)), dma((7,)), dma((7,)), dma((7,)), dma((7,)), dma((7,)),
            dma((12, 3)), dma((12, 3)), dma((12,)), dma((12,)), dma((4,)), dma((4,)),
            dma((PANELS, PEERS - 1)), dma((PANELS, PEERS - 1)), dma((2 * PANELS,)),
            dma((PANELS, SENDS)), dma((PANELS, len(ROLES))),
        ],
        compiler_params=pltpu.CompilerParams(
            vmem_limit_bytes=63 << 20, collective_id=0, has_side_effects=True
        ),
        name="scores",
    )(query, train, slot, owner, count)
    return scores


def body(query_gradient_stack, train_grads, factor_slots, owner, train_count):
    slot = factor_slots.reshape(PANELS, PEERS, STRIP, PANEL)
    return scores_of(query_gradient_stack[0], train_grads[0], slot, owner, train_count)[None]


def solution(mesh):
    in_specs = (
        P("section", "dp", None),
        P("section", "dp", None),
        P("section", "dp", None, None),
        P("section", None),
        P("dp"),
    )
    out_specs = P("dp", "section", None)
    return jax.shard_map(body, mesh=mesh, in_specs=in_specs, out_specs=out_specs, check_vma=False)
```

time: 306 us -> 180 us (0.59)
  waiting for transfers between devices: 152 us -> 0 us
  Pallas kernels: 123 us -> 177 us
  between operations: 16.6 us -> 0.66 us
  other arithmetic: 10.2 us -> 0 us
    psum x1 -> x0, waiting for transfers between devices: 152 us -> none  [spread(): return lax.psum(block, axis)]
    pallas_call x1, Pallas kernels: 123 us -> 177 us  [scores_of(): pl.pallas_call(score_kernel, out_shape=(jax.ShapeDtypeStruct((64, 3 * ROW...]
    select_n x4 -> x0, other arithmetic: 10.2 us -> none  [spread(): jnp.where(lax.axis_index(axis) == source, block, jnp.zeros_like(block))]
  transfers between devices with their start and end apart: 1 -> 0, of which waited for: 1 -> 0; matrix products, arithmetic and copies ran while one was open for 0% -> 0% of each run, Pallas kernels for 0% -> 0%
where the time goes in v3:
time: 180 us; the launch traced here: 179 us
  Pallas kernels  177 us (98%)
    pallas_call x1, Pallas kernels, scores_of(): pl.pallas_call(score_kernel, out_shape=(jax.ShapeDtypeStruct((64, 3 * ROW...  177 us

profile of v3, /device:TPU:0, one launch (start us, length us, event | category | flops | bytes accessed | tf_op | source)
XLA Modules:
  0.0 179.4 jit_solution(1238976687409602884)
XLA Ops:
  0.7 177.0 %scores.1 = (f32[64,1536]{1,0:T(8,128)}, f32[10,16,32,512]{3,2,1,0:T(8,128)}) custom-call(f32[512,2048]{1,0:T(8,128)} %bitcast.4, f32[512,2048]{1,0:T(8,128)} %bitcast.5, f32[4,16,32,512]{3,2,1,0:T(8,128)} %bitcast.6, s32[1,4]{1,0:T(1,128)} %owner_ref.1, s32[1]{0:T(128)S(6)} %copy.7.count_ref), custom_call_target="tpu_custom_call" | custom-call | tf_op jit(solution)/shard_map/scores/pallas_call | solution.py:617
  177.6 1.8 copy.8

commit v4 on v3

--- a/solution.py
+++ b/solution.py
@@ -21,6 +21,7 @@
 PEERS = 16
 STRIP = PANEL // PEERS
 Z_ROWS = STRIP // 2
+EARLY = 2
 PIECES = [group * (group + 1) // 2 for group in range(PANELS + 1)]
 
 
@@ -150,12 +151,15 @@
 
 
 class Exchange:
-    def __init__(self, slot, owner, factor, gathered, mine, sems):
+    def __init__(self, slot, owner, factor, gathered, chosen, pair, mine, sems):
+        self.chosen, self.pair = chosen, pair
         self.slot, self.owner, self.factor, self.gathered, self.mine = slot, owner, factor, gathered, mine
-        self.spread_send, self.spread_recv, self.local, self.pass_send, self.pass_recv = sems
+        self.spread_send, self.spread_recv, self.local, self.pass_send, self.pass_recv, self.pair_sems = sems
         me = self.me = lax.axis_index("dp")
         self.z, self.x, self.core = z, x, core = me // 8, (me // 2) % 4, me % 2
         order = ((1, 0), (0, 1), (1, 3), (0, 2), (1, 1), (0, 3), (1, 2), (0, 0))
+        steps = [(dz, dx, dc) for dz, dx in order for dc in (0, 1) if dz or dx or dc]
+        self.same_core = [number for number, step in enumerate(steps) if step[2] == 0]
         self.peers = [
             device_at(z + dz, x + dx, core + dc) for dz, dx in order for dc in (0, 1) if dz or dx or dc
         ]
@@ -172,14 +176,44 @@
             device_id={"dp": where}, device_id_type=MESH,
         )
 
+    def pair_send(self):
+        return self.remote(
+            self.slot.at[0, :, 1 - self.core], self.pair, self.pair_sems.at[0], self.pair_sems.at[1], self.other
+        )
+
+    def pair_own(self):
+        return pltpu.make_async_copy(self.slot.at[0, :, self.core], self.chosen, self.pair_sems.at[2])
+
+    def pair_start(self):
+        self.pair_send().start()
+        self.pair_own().start()
+
+    def pair_pick(self):
+        self.pair_send().wait()
+        self.pair_own().wait()
+        self.chosen[...] = jnp.where(self.owner[0, 0] == self.me, self.chosen[...], self.pair[...])
+
+    def spread_first(self):
+        chip = self.me // 2
+        for number, to in enumerate(self.peers):
+            if number in self.same_core:
+                yield self.remote(
+                    self.chosen.at[to // 2], self.gathered[0].at[chip],
+                    self.spread_send.at[0, number], self.spread_recv.at[0, number], to,
+                )
+        yield pltpu.make_async_copy(self.chosen.at[chip], self.gathered[0].at[chip], self.local.at[0])
+
     def spread(self, group):
+        if group == 0:
+            yield from self.spread_first()
+            return
         for number, to in enumerate(self.peers):
             yield self.remote(
-                self.slot.at[group, to], self.gathered[group].at[self.me],
+                self.slot.at[group, to // 2, to % 2], self.gathered[group].at[self.me],
                 self.spread_send.at[group, number], self.spread_recv.at[group, number], to,
             )
         yield pltpu.make_async_copy(
-            self.slot.at[group, self.me], self.gathered[group].at[self.me], self.local.at[group]
+            self.slot.at[group, self.me // 2, self.core], self.gathered[group].at[self.me], self.local.at[group]
         )
 
     def spread_start(self, group):
@@ -190,7 +224,8 @@
         for copy in self.spread(group):
             copy.wait()
         for number in range(group + 1):
-            self.mine[PIECES[group] + number] = self.gathered[group][self.owner[0, number]]
+            source = self.owner[0, number] if group else lax.div(self.owner[0, number], 2)
+            self.mine[PIECES[group] + number] = self.gathered[group][source]
 
     def pieces(self, group):
         return slice(PIECES[group], PIECES[group + 1])
@@ -271,9 +306,9 @@
 
 def score_kernel(
     q_hbm, t_hbm, slot_hbm, owner_ref, count_ref, out_ref, factor,
-    gather_0, gather_1, gather_2, gather_3, mine,
+    gather_0, gather_1, gather_2, gather_3, chosen, pair, mine,
     l_high, l_low, x_ref, x_high, x_low, w_high, w_low, stage,
-    a_in, b_in, tiles, first_in, second_out, second_in, kept, third_out, third_in,
+    a_in, b_in, tiles, first_in, second_out, second_in, kept, third_in,
     load_sem, stage_sem, a_send, a_recv, b_send, b_recv, r_send,
     f_send, f_recv, s_send, s_recv, m_send, m_recv, *pass_sems,
 ):
@@ -285,7 +320,7 @@
     after, before_two = lax.rem(me + 1, count), lax.rem(me + count - 2, count)
     after_two = lax.rem(me + 2, count)
     exchange = Exchange(
-        slot_hbm, owner_ref, factor, (gather_0, gather_1, gather_2, gather_3), mine, pass_sems
+        slot_hbm, owner_ref, factor, (gather_0, gather_1, gather_2, gather_3), chosen, pair, mine, pass_sems
     )
 
     def section_at(steps):
@@ -297,6 +332,9 @@
         pl.semaphore_signal(barrier, inc=1, device_id={"dp": other}, device_id_type=MESH)
     for other in (section_at(1), section_at(2), section_at(3), partner):
         pl.semaphore_signal(barrier, inc=1, device_id={"section": other}, device_id_type=MESH)
+    pl.semaphore_signal(
+        barrier, inc=1, device_id={"dp": before_two, "section": partner}, device_id_type=MESH
+    )
 
     copies = [
         pltpu.make_async_copy(source, x_ref.at[index], load_sem.at[index])
@@ -304,9 +342,12 @@
     ]
     for copy in copies:
         copy.start()
-    pl.semaphore_wait(barrier, len(exchange.peers) + 4)
+    pl.semaphore_wait(barrier, len(exchange.peers) + 5)
+    exchange.pair_start()
+    exchange.spread_start(1)
+    exchange.pair_pick()
     exchange.spread_start(0)
-    exchange.spread_start(1)
+    exchange.spread_start(2)
     for copy in copies:
         copy.wait()
     place = lax.broadcasted_iota(jnp.int32, (ROWS, SMALL), 0)
@@ -321,7 +362,8 @@
             device_id=where, device_id_type=MESH,
         )
 
-    whole, early, last = pl.ds(0, ROWS), slice(0, COORDS - PANEL), pl.ds(COORDS - PANEL, PANEL)
+    whole, early = pl.ds(0, ROWS), slice(0, EARLY * PANEL)
+    last = pl.ds(EARLY * PANEL, COORDS - EARLY * PANEL)
 
     def chunk(part):
         return pl.ds(pl.multiple_of(part * CHUNK, CHUNK), CHUNK)
@@ -369,8 +411,8 @@
     for group in range(PANELS):
         exchange.spread_wait(group)
         exchange.stage_0(group)
-        if group + 2 < PANELS:
-            exchange.spread_start(group + 2)
+        if group == 0:
+            exchange.spread_start(3)
         if group >= 1:
             exchange.stage_1(group - 1)
         if group >= 2:
@@ -383,18 +425,17 @@
     exchange.stage_1(3)
     exchange.stage_2(2)
     exchange.stage_3(1)
-    shift_group(0)
     exchange.arrived(1)
     load(1)
     exchange.stage_2(3)
     exchange.stage_3(2)
     solve_both(1)
     exchange.stage_3(3)
+    shift_group(0)
     shift_group(1)
     exchange.arrived(2)
     load(2)
     solve_both(2)
-    shift_group(2)
     exchange.arrived(3)
     load(3)
 
@@ -489,36 +530,36 @@
             else:
                 second_out[2, small_rows(part, 0), :] = total
         second_row(part).start()
+        move(part).start()
 
     def second_row(part):
         at = 8 + part
         return remote(
             second_out.at[2, small_rows(part, 0), :], second_in.at[2, small_rows(part, 0), :],
-            s_send.at[at], s_recv.at[at], {"section": partner},
+            s_send.at[at], s_recv.at[at], {"dp": after_two, "section": partner},
         )
 
     def move(part):
         return remote(
-            third_out.at[small_rows(part, 0), :], third_in.at[small_rows(part, 0), :],
+            kept.at[2, small_rows(part, 0), :], third_in.at[small_rows(part, 0), :],
             m_send.at[part], m_recv.at[part], {"dp": after_two},
         )
 
     def end_rows(part):
         second_row(part).wait()
+        move(part).wait()
         rows = small_rows(part, 0)
-        third_out[rows, :] = kept[2, rows, :] + second_in[2, rows, :]
-        move(part).start()
-
-    relay_group(0)
-    relay_group(1)
+        out_ref[rows, 2 * ROWS :] = third_in[rows, :] + second_in[2, rows, :]
+
+    for group in range(EARLY):
+        relay_group(group)
     tiles[0] = dot3(x_high[0], x_low[0], x_high[1], x_low[1])
     for part in range(4):
         for steps in (1, 2, 3):
             first_column(0, part, steps).start()
-    relay_group(2)
     keep_split(a_in, 0)
     tiles[1] = dot3(x_high[0, :, early], x_low[0, :, early], l_high[:ROWS, early], l_low[:ROWS, early])
-    for group in range(PANELS - 1):
+    for group in range(EARLY):
         view = b_in.at[whole, group_cols(group)]
         pltpu.make_async_copy(view, view, b_recv.at[group]).wait()
     keep_split(b_in, ROWS)
@@ -532,17 +573,23 @@
     def _():
         tiles[2] = dot3(l_high[second, early], l_low[second, early], x_high[1, :, early], x_low[1, :, early])
 
-    @pl.loop(0, 7)
+    @pl.when(odd)
+    def _():
+        @pl.loop(0, 4)
+        def _(part):
+            send_train(3 + part, chunk(part), last).wait()
+            column_piece(1, part, a_in)
+
+    @pl.loop(0, 6)
     def _(step):
         @pl.when(step < 4)
         def _():
-            send_train(3 + step, chunk(step), last).wait()
-
             @pl.when(even)
             def _():
+                send_train(3 + step, chunk(step), last).wait()
                 relay(3 + step, chunk(step), last).start()
-
-            column_piece(1, step, a_in)
+                column_piece(1, step, a_in)
+
             view = b_in.at[chunk(step), last]
             pltpu.make_async_copy(view, view, b_recv.at[3 + step]).wait()
 
@@ -589,14 +636,9 @@
             def _():
                 end_rows(step - 2)
 
-        @pl.when((step >= 3) & even)
-        def _():
-            move(step - 3).wait()
-            out_ref[small_rows(step - 3, 0), 2 * ROWS :] = third_in[small_rows(step - 3, 0), :]
-
     @pl.when(even)
     def _():
-        for group in range(PANELS - 1):
+        for group in range(EARLY):
             relay(group, whole, group_cols(group)).wait_send()
             send_query(group, whole, group_cols(group)).wait_send()
         for part in range(4):
@@ -604,7 +646,7 @@
             view = b_in.at[chunk(part), last]
             pltpu.make_async_copy(view, view, b_send.at[3 + part]).wait()
 
-    for group in range(PANELS - 1):
+    for group in range(EARLY):
         send_train(group, whole, group_cols(group)).wait_send()
 
     exchange.drain()
@@ -622,8 +664,11 @@
         ),
         in_specs=[anyspace] * 3 + [smem] * 2,
         out_specs=(vmem, anyspace),
-        scratch_shapes=[pltpu.VMEM((PEERS, STRIP, PANEL), F32)] * PANELS
+        scratch_shapes=[pltpu.VMEM((PEERS // 2, STRIP, PANEL), F32)]
+        + [pltpu.VMEM((PEERS, STRIP, PANEL), F32)] * (PANELS - 1)
         + [
+            pltpu.VMEM((PEERS // 2, STRIP, PANEL), F32),
+            pltpu.VMEM((PEERS // 2, STRIP, PANEL), F32),
             pltpu.VMEM((PIECES[-1], STRIP, PANEL), F32),
             pltpu.VMEM((COORDS, COORDS), BF16),
             pltpu.VMEM((COORDS, COORDS), BF16),
@@ -641,11 +686,10 @@
             pltpu.VMEM((3, 64, ROWS), F32),
             pltpu.VMEM((3, 64, ROWS), F32),
             pltpu.VMEM((64, ROWS), F32),
-            pltpu.VMEM((64, ROWS), F32),
             dma((2,)), dma((2,)), dma((7,)), dma((7,)), dma((7,)), dma((7,)), dma((7,)),
             dma((12, 3)), dma((12, 3)), dma((12,)), dma((12,)), dma((4,)), dma((4,)),
             dma((PANELS, PEERS - 1)), dma((PANELS, PEERS - 1)), dma((2 * PANELS,)),
-            dma((PANELS, SENDS)), dma((PANELS, len(ROLES))),
+            dma((PANELS, SENDS)), dma((PANELS, len(ROLES))), dma((3,)),
         ],
         compiler_params=pltpu.CompilerParams(
             vmem_limit_bytes=63 << 20, collective_id=0, has_side_effects=True
@@ -656,7 +700,7 @@
 
 
 def body(query_gradient_stack, train_grads, factor_slots, owner, train_count):
-    slot = factor_slots.reshape(PANELS, PEERS, STRIP, PANEL)
+    slot = factor_slots.reshape(PANELS, PEERS // 2, 2, STRIP, PANEL)
     return scores_of(query_gradient_stack[0], train_grads[0], slot, owner, train_count)[None]
 
 

time: 180 us -> 162 us (0.900)
  Pallas kernels: 177 us -> 159 us
    pallas_call x1, Pallas kernels: 177 us -> 159 us  [scores_of(): pl.pallas_call(score_kernel, out_shape=(jax.ShapeDtypeStruct((64, 3 * ROW...]
where the time goes in v4:
time: 162 us; the launch traced here: 161 us
  Pallas kernels  159 us (98%)
  local copies, waits for them, and re-layouts  1.77 us (1%)
    pallas_call x1, Pallas kernels, scores_of(): pl.pallas_call(score_kernel, out_shape=(jax.ShapeDtypeStruct((64, 3 * ROW...  159 us

profile of v4, /device:TPU:0, one launch (start us, length us, event | category | flops | bytes accessed | tf_op | source)
XLA Modules:
  0.0 161.2 jit_solution(6332203010876568496)
XLA Ops:
  0.7 158.8 %scores.1 = (f32[64,1536]{1,0:T(8,128)}, f32[10,16,32,512]{3,2,1,0:T(8,128)}) custom-call(f32[512,2048]{1,0:T(8,128)} %bitcast.4, f32[512,2048]{1,0:T(8,128)} %bitcast.5, f32[4,8,2,32,512]{4,3,2,1,0:T(8,128)} %bitcast.6, s32[1,4]{1,0:T(1,128)} %owner_ref.1, s32[1]{0:T(128)S(6)} %copy.7.count_ref), custom_call_target="tpu_custom_call" | custom-call | tf_op jit(solution)/shard_map/scores/pallas_call | solution.py:659
  159.4 1.8 %copy.8 = f32[1,64,1536]{2,1,0:T(8,128)} copy(f32[1,64,1536]{2,1,0:T(8,128)} %bitcast.7) | data formatting | bytes 786432
